TPU v7x, 32 devices: a whole 2x2x4 slice. The times are simulated.
32 devices in a mesh: expert: 16 (over z, y, x), replica: 2 (over core).
Axes of the slice: x: 2, y: 2, z: 4, core: 2. Of those that a mesh axis runs over, the one named last changes fastest.
Arguments:
- tokens: bfloat16 [2048, 1024], P(('expert', 'replica')), may hold values from -6 to 6
- route_ids: int32 [2048, 6], P(('expert', 'replica')), may hold values from 0 to 15, all different within a row; in each aligned block of 64 rows (0 to 63, 64 to 127, ...) at most 28 rows name the same one
- route_weights: bfloat16 [2048, 6], P(('expert', 'replica')), may hold values from 0.049804688 to 0.5
- out_grad: bfloat16 [2048, 1024], P(('expert', 'replica')), may hold values from -3 to 3
- w_gate: bfloat16 [16, 1024, 384], P('expert'), may hold values from -0.1875 to 0.1875
- w_up: bfloat16 [16, 1024, 384], P('expert'), may hold values from -0.1875 to 0.1875
- w_down: bfloat16 [16, 1024, 384], P('expert'), may hold values from -0.3125 to 0.3125
- mom_gate: float32 [16, 1024, 384], P('expert', 'replica'), may hold values from -6 to 6
- mom_up: float32 [16, 1024, 384], P('expert', 'replica'), may hold values from -6 to 6
- mom_down: float32 [16, 1024, 384], P('expert', 'replica'), may hold values from -6 to 6
Outputs:
- grad_tokens: bfloat16 [2048, 1024], P(('expert', 'replica'))
- grad_route: bfloat16 [2048, 6], P(('expert', 'replica'))
- new_gate: float32 [16, 1024, 384], P('expert', 'replica')
- new_up: float32 [16, 1024, 384], P('expert', 'replica')
- new_down: float32 [16, 1024, 384], P('expert', 'replica')
Inputs may be any that keep to these rules, and one draw needn't show every extreme that they name: `route_ids`: each row names 6 different experts. Among the 64 rows of one device no expert is named more than 28 times, a bound that some block reaches.
All inputs are finite; a program needn't handle non-finite values.
Results may differ from a plain program's by a relative error of at most 0.015.
Values may be sent and summed in bfloat16 or wider, within the bound.
No kernel may reach another device: no remote copies, remote signals or barrier semaphores. Data moves between devices by JAX's collectives and lax.ppermute only.
A program may use at most 64 MiB of HBM per device.

v0:
```python
import functools

import jax
import jax.numpy as jnp
from jax import lax
from jax.experimental import pallas as pl
from jax.experimental.pallas import tpu as pltpu
from jax.sharding import PartitionSpec as P


F32 = jnp.float32
BF16 = jnp.bfloat16
ROWS_BY_ROWS = (((0,), (0,)), ((), ()))
COLS_BY_COLS = (((1,), (1,)), ((), ()))
VMEM = pl.BlockSpec(memory_space=pltpu.VMEM)
SMEM = pl.BlockSpec(memory_space=pltpu.SMEM)


ANY = pl.BlockSpec(memory_space=pl.ANY)


def call(kernel, outs, ins, flops, scratch=(), streamed=(), out_streamed=(), limit=32):
    nbytes = sum(x.size * x.dtype.itemsize for x in list(ins[1:]) + list(outs))
    return pl.pallas_call(
        kernel,
        out_shape=tuple(outs),
        in_specs=[SMEM] + [ANY if i in streamed else VMEM for i in range(1, len(ins))],
        out_specs=tuple(ANY if i in out_streamed else VMEM for i in range(len(outs))),
        scratch_shapes=list(scratch),
        cost_estimate=pl.CostEstimate(flops=flops, bytes_accessed=nbytes, transcendentals=0),
        compiler_params=pltpu.CompilerParams(vmem_limit_bytes=limit << 20),
    )(*ins)


class Layout:
    def __init__(self, cap):
        self.cap = cap
        self.whole = cap // 8 * 8
        self.rest = cap - self.whole
        self.mixed = -(-2 * self.rest // 8) * 8
        self.rows = 2 * self.whole + self.mixed
        self.side = self.whole + self.mixed

    def row(self, slot, second):
        late = slot >= self.whole
        first_row = slot + jnp.where(late, 1.0 * self.whole, 0.0)
        second_row = slot + jnp.where(late, 1.0 * (self.whole + self.rest), 1.0 * self.whole)
        return jnp.where(second, second_row, first_row)


def selection(key, value, chunk):
    experts, lanes = key.shape
    slot = lax.broadcasted_iota(jnp.int32, (experts, chunk, lanes), 1)
    hit = slot == key.astype(jnp.int32)[:, None, :]
    full = jnp.where(hit, jnp.broadcast_to(value[:, None, :], hit.shape), 0.0)
    return full.reshape(experts * chunk, lanes).astype(BF16)


def pack(key, value, both, chunk, staged, packed, sems):
    copies = []
    for e in range(key.shape[0]):
        pick = selection(key[e : e + 1], value[e : e + 1], chunk)
        staged[e] = jnp.dot(pick, both, preferred_element_type=F32).astype(BF16)
        copies.append(pltpu.make_async_copy(staged.at[e], packed.at[e], sems.at[e]))
        copies[-1].start()
    for copy in copies:
        copy.wait()


def route_kernel(
    lay, where, ids_in, weights_in, tok, grad, packed, table, far,
    ids, weights, both, staged, in_sems, sems,
):
    rows = tok.shape[0]
    loads = [
        pltpu.make_async_copy(ids_in, ids, in_sems.at[0]),
        pltpu.make_async_copy(weights_in, weights, in_sems.at[1]),
        pltpu.make_async_copy(tok, both.at[pl.ds(0, rows)], in_sems.at[2]),
        pltpu.make_async_copy(grad, both.at[pl.ds(rows, rows)], in_sems.at[3]),
    ]
    for load in loads:
        load.start()
    topk = ids.shape[0]
    experts, lanes = table.shape[1], table.shape[2]
    sub = experts // 2
    source = lax.broadcasted_iota(jnp.int32, (rows, lanes), 0)
    lane = lax.broadcasted_iota(jnp.int32, (rows, lanes), 1)
    target = jnp.where(lane >= rows, lane - rows, lane)
    earlier = jnp.where(source < target, 1.0, 0.0).astype(BF16)
    same = jnp.where(source == target, 1.0, 0.0).astype(BF16)
    expert = lax.broadcasted_iota(jnp.int32, (experts, rows), 0)
    named = jnp.zeros((experts, rows), F32)
    weight = jnp.zeros((experts, rows), F32)
    loads[0].wait()
    loads[1].wait()
    for k in range(topk):
        hit = ids[k : k + 1, :] == expert
        named = named + jnp.where(hit, 1.0, 0.0)
        weight = weight + jnp.where(hit, weights[k : k + 1, :].astype(F32), 0.0)
    named_b = named.astype(BF16)
    position = jnp.dot(named_b, earlier, preferred_element_type=F32)
    present = jnp.dot(named_b, same, preferred_element_type=F32)
    factor = jnp.dot(weight.astype(BF16), same, preferred_element_type=F32)
    second = lax.broadcasted_iota(jnp.int32, (experts, lanes), 1) >= rows
    table[0] = jnp.where(present > 0.5, lay.row(position, second), -1.0)
    table[1] = jnp.where(second, factor, 1.0)
    own = pl.ds(pl.multiple_of(where[0] * sub, sub), sub)
    other = pl.ds(pl.multiple_of((1 - where[0]) * sub, sub), sub)
    far[0] = table[0, other, :]
    far[1] = table[1, other, :]
    loads[2].wait()
    loads[3].wait()
    pack(table[0, own, :], table[1, own, :], both[...], lay.rows, staged, packed, sems)


def relay_kernel(lay, where, far, tok, grad, packed, staged, sems):
    both = jnp.concatenate([tok[...], grad[...]], axis=0)
    pack(far[0], far[1], both, lay.rows, staged, packed, sems)


def split_sides(lay, got, first, second):
    for e in range(got.shape[0]):
        at, side, whole = e * lay.side, lay.side, lay.whole
        if whole:
            first[at : at + whole] = got[e, :whole]
            second[at : at + whole] = got[e, whole : 2 * whole]
        first[at + whole : at + side] = got[e, 2 * whole :]
        second[at + whole : at + side] = got[e, 2 * whole :]


def align(lay, x, experts):
    parts = []
    for e in range(experts):
        at = e * lay.side
        if lay.whole:
            parts.append(x[at : at + lay.whole])
        late = x[at + lay.whole : at + lay.side]
        parts.append(pltpu.roll(late, lay.mixed - lay.rest, 0) if lay.rest else late)
    return jnp.concatenate(parts, axis=0)


def expert_kernel(
    lay, where, got, gate_in, up_in, down_in, back_rows, first, second, small, down_small, sums,
    w_gate, w_up, w_down, staged, in_sems, sems,
):
    loads = [
        pltpu.make_async_copy(gate_in, w_gate, in_sems.at[0]),
        pltpu.make_async_copy(up_in, w_up, in_sems.at[1]),
        pltpu.make_async_copy(down_in, w_down, in_sems.at[2]),
    ]
    for load in loads:
        load.start()
    sub, _, width = got.shape
    units = w_gate.shape[1]
    total = sub * lay.side
    split_sides(lay, got, first, second)
    loads[0].wait()
    gate = jnp.dot(first[...], w_gate[...], preferred_element_type=F32)
    loads[1].wait()
    up = jnp.dot(first[...], w_up[...], preferred_element_type=F32)
    loads[2].wait()
    back = jnp.dot(second[...], w_down[...], preferred_element_type=F32)
    back = align(lay, back, sub)
    slot = lax.broadcasted_iota(jnp.int32, (sub, lay.side, 128), 1).reshape(total, 128)
    filled = slot[:, :1] < lay.cap
    sig = 1.0 / (1.0 + jnp.exp(-gate))
    act = gate * sig
    hidden = jnp.where(filled, act * up, 0.0)
    grad_gate = jnp.where(filled, back * up * sig * (1.0 + gate * (1.0 - sig)), 0.0).astype(BF16)
    grad_up = jnp.where(filled, back * act, 0.0).astype(BF16)
    slot_grad = lax.dot_general(grad_gate, w_gate[...], COLS_BY_COLS, preferred_element_type=F32)
    slot_grad = slot_grad + lax.dot_general(
        grad_up, w_up[...], COLS_BY_COLS, preferred_element_type=F32
    )
    half = width // 2
    copies = []
    early = lax.broadcasted_iota(jnp.int32, (lay.mixed, half), 0) < lay.rest
    for e in range(sub):
        at, whole = e * lay.side, lay.whole
        if whole:
            staged[e, :whole] = slot_grad[at : at + whole, :half].astype(BF16)
            staged[e, whole : 2 * whole] = slot_grad[at : at + whole, half:].astype(BF16)
        late = slot_grad[at + whole : at + lay.side]
        if lay.rest:
            mixed = jnp.where(early, late[:, :half], pltpu.roll(late[:, half:], lay.rest, 0))
            staged[e, 2 * whole :] = mixed.astype(BF16)
        copies.append(pltpu.make_async_copy(staged.at[e], back_rows.at[e], sems.at[e]))
        copies[-1].start()
    small[:, :units] = grad_gate
    small[:, units:] = grad_up
    parts = []
    for e in range(sub):
        at, whole = e * lay.side, lay.whole
        if whole:
            parts.append(hidden[at : at + whole])
        late = hidden[at + whole : at + lay.side]
        parts.append(pltpu.roll(late, lay.rest, 0) if lay.rest else late)
    down_small[...] = jnp.concatenate(parts, axis=0).astype(BF16)
    route = jnp.sum(hidden * back, axis=1, keepdims=True)
    lane = lax.broadcasted_iota(jnp.int32, (total, 128), 1)
    spread = jnp.where(lane == slot, route, 0.0).reshape(sub, lay.side, 128)
    sums[...] = jnp.sum(spread, axis=1)
    for copy in copies:
        copy.wait()


def weight_parts(where, first, second, small, down_small, turned, replicas):
    width = first.shape[1] // replicas
    for b in range(replicas):
        turned[0, b] = first[:, b * width : (b + 1) * width]
        turned[1, b] = second[:, b * width : (b + 1) * width]
    for s in range(replicas):
        b = lax.rem(where[1] + s, replicas)
        upper = lax.dot_general(
            turned[0, b], small[...], ROWS_BY_ROWS, preferred_element_type=F32
        )
        lower = lax.dot_general(
            turned[1, b], down_small[...], ROWS_BY_ROWS, preferred_element_type=F32
        )
        yield s, upper, lower


def weight_a_kernel(where, first, second, small, down_small, out, turned):
    columns = small.shape[1]
    for s, upper, lower in weight_parts(
        where, first, second, small, down_small, turned, out.shape[0]
    ):
        out[s, :, :columns] = upper
        out[s, :, columns:] = lower


def weight_b_kernel(replicas, where, first, second, small, down_small, part, *rest):
    outs, turned = rest[:replicas], rest[replicas]
    columns = small.shape[1]
    for s, upper, lower in weight_parts(
        where, first, second, small, down_small, turned, replicas
    ):
        outs[s][:, :columns] = (part[s, :, :columns] + upper).astype(BF16)
        outs[s][:, columns:] = (part[s, :, columns:] + lower).astype(BF16)


def update_kernel(replicas, *refs):
    parts, moms, outs = refs[:replicas], refs[replicas : replicas + 3], refs[replicas + 3 :]
    units = moms[0].shape[2]
    for i in range(3):
        cols = slice(i * units, (i + 1) * units)
        total = parts[0][:, cols].astype(F32)
        for part in parts[1:]:
            total = total + part[:, cols].astype(F32)
        outs[i][0] = 0.9 * moms[i][0] + 0.1 * total


def gathered(key, returned, chunk):
    ones = jnp.ones(key.shape, F32)
    flat = returned.reshape(returned.shape[0] * returned.shape[1], returned.shape[2])
    return lax.dot_general(
        selection(key, ones, chunk), flat, ROWS_BY_ROWS, preferred_element_type=F32
    )


def partial_kernel(lay, where, far, returned, out):
    rows, half = out.shape[0], returned.shape[2]
    total = gathered(far[0], returned[...], lay.rows)
    out[:, :half] = total[:rows].astype(BF16)
    out[:, half:] = total[rows:].astype(BF16)


def final_kernel(lay, where, table, returned, partial, sums, ids, weights, out, route):
    rows, half = out.shape[0], returned.shape[2]
    topk = ids.shape[0]
    experts = table.shape[1]
    sub = experts // 2
    own = pl.ds(pl.multiple_of(where[0] * sub, sub), sub)
    total = gathered(table[0, own, :], returned[...], lay.rows)
    out[:, :half] = (total[:rows] + partial[:, :half].astype(F32)).astype(BF16)
    out[:, half:] = (total[rows:] + partial[:, half:].astype(F32)).astype(BF16)
    key = table[0]
    key = jnp.where(key >= lay.whole, key - lay.whole, key).astype(jnp.int32)
    value = jnp.zeros(key.shape, F32)
    per_slot = sums[:, 0, :]
    for q in range(lay.cap):
        value = value + jnp.where(key == q, per_slot[:, q : q + 1], 0.0)
    value = value[:, :rows]
    expert = lax.broadcasted_iota(jnp.int32, (experts, rows), 0)
    for k in range(topk):
        picked = jnp.sum(
            jnp.where(ids[k : k + 1, :] == expert, value, 0.0), axis=0, keepdims=True
        )
        route[k : k + 1, :] = (picked / weights[k : k + 1, :].astype(F32)).astype(BF16)


def per_device(
    tokens, route_ids, route_weights, out_grad, w_gate, w_up, w_down, mom_gate, mom_up, mom_down
):
    experts = lax.axis_size("expert")
    replicas = lax.axis_size("replica")
    rows, width = tokens.shape
    topk = route_ids.shape[1]
    units = w_gate.shape[2]
    lay = Layout(7 * rows * topk // (6 * experts))
    sub = experts // 2
    lanes = 2 * rows
    half = width // 2
    strip = width // replicas
    total = sub * lay.side
    place = lax.axis_index("expert") // sub
    where = jnp.stack([place, lax.axis_index("replica")]).astype(jnp.int32)
    groups = [list(range(sub)), list(range(sub, experts))]
    S = jax.ShapeDtypeStruct
    DMA = pltpu.SemaphoreType.DMA

    def across(x):
        return lax.ppermute(
            x, "expert", [(i, (i + sub) % experts) for i in range(experts)]
        )

    def within(x):
        return lax.all_to_all(
            x, "expert", split_axis=0, concat_axis=0, tiled=True, axis_index_groups=groups
        )

    ids = route_ids.T
    weights = route_weights.T
    far_tok = across(tokens)
    far_grad = across(out_grad)
    chunks = S((sub, lay.rows, width), BF16)
    staged = pltpu.VMEM(chunks.shape, BF16)
    packed, table, far = call(
        functools.partial(route_kernel, lay),
        [chunks, S((2, experts, lanes), F32), S((2, sub, lanes), F32)],
        (where, ids, weights, tokens, out_grad),
        2 * sub * lay.rows * lanes * width,
        scratch=[
            pltpu.VMEM(ids.shape, ids.dtype),
            pltpu.VMEM(weights.shape, weights.dtype),
            pltpu.VMEM((2 * rows, width), BF16),
            staged,
            DMA((4,)),
            DMA((sub,)),
        ],
        streamed=(1, 2, 3, 4),
        out_streamed=(0,),
        limit=16,
    )
    far = across(far)
    got_a = within(packed)
    (relayed,) = call(
        functools.partial(relay_kernel, lay),
        [chunks],
        (where, far, far_tok, far_grad),
        2 * sub * lay.rows * lanes * width,
        scratch=[staged, DMA((sub,))],
        out_streamed=(0,),
        limit=16,
    )
    got_b = within(relayed)

    def expert(got):
        weight = pltpu.VMEM((width, units), BF16)
        return call(
            functools.partial(expert_kernel, lay),
            [
                S((sub, lay.rows, half), BF16),
                S((total, width), BF16),
                S((total, width), BF16),
                S((total, 2 * units), BF16),
                S((total, units), BF16),
                S((sub, 128), F32),
            ],
            (where, got, w_gate[0], w_up[0], w_down[0]),
            10 * total * width * units,
            scratch=[weight, weight, weight, pltpu.VMEM((sub, lay.rows, half), BF16)]
            + [DMA((3,)), DMA((sub,))],
            streamed=(2, 3, 4),
            out_streamed=(0,),
        )

    back_a, *factors_a, sums_a = expert(got_a)
    turned = pltpu.VMEM((2, replicas, total, strip), BF16)
    (part_a,) = call(
        weight_a_kernel,
        [S((replicas, strip, 3 * units), F32)],
        (where, *factors_a),
        6 * total * width * units,
        scratch=[turned],
    )
    back_b, *factors_b, sums_b = expert(got_b)
    ret_b = within(back_b)
    ret_a = within(back_a)
    parts = call(
        functools.partial(weight_b_kernel, replicas),
        [S((strip, 3 * units), BF16)] * replicas,
        (where, *factors_b, part_a),
        6 * total * width * units,
        scratch=[turned],
    )
    moved = [
        lax.ppermute(
            parts[s], "replica", [(i, (i + s) % replicas) for i in range(replicas)]
        )
        for s in range(1, replicas)
    ]
    (partial,) = call(
        functools.partial(partial_kernel, lay),
        [S((rows, width), BF16)],
        (where, far, ret_b),
        2 * sub * lay.rows * lanes * half,
        limit=16,
    )
    partial = across(partial)
    sums = jnp.where(
        place == 0,
        jnp.concatenate([sums_a, sums_b], axis=0),
        jnp.concatenate([sums_b, sums_a], axis=0),
    )
    sums = jnp.broadcast_to(sums[:, None, :], (experts, 8, 128))
    sums = lax.all_to_all(sums, "expert", split_axis=0, concat_axis=0, tiled=True)
    block = min(128, strip)
    mom_spec = pl.BlockSpec((1, block, units), lambda i: (0, i, 0))
    part_spec = pl.BlockSpec((block, 3 * units), lambda i: (i, 0))
    new = pl.pallas_call(
        functools.partial(update_kernel, replicas),
        grid=(strip // block,),
        out_shape=[S(mom_gate.shape, F32)] * 3,
        in_specs=[part_spec] * replicas + [mom_spec] * 3,
        out_specs=[mom_spec] * 3,
        cost_estimate=pl.CostEstimate(
            flops=9 * strip * units,
            bytes_accessed=24 * strip * units + 6 * replicas * strip * units,
            transcendentals=0,
        ),
        compiler_params=pltpu.CompilerParams(vmem_limit_bytes=16 << 20),
        name="update",
    )(parts[0], *moved, mom_gate, mom_up, mom_down)
    grad_tokens, grad_route = call(
        functools.partial(final_kernel, lay),
        [S((rows, width), BF16), S((topk, rows), BF16)],
        (where, table, ret_a, partial, sums, ids, weights),
        2 * sub * lay.rows * lanes * half,
        limit=16,
    )
    return (grad_tokens, grad_route.T, *new)


def solution(mesh):
    tok = P(("expert", "replica"), None)
    full = P("expert", None, None)
    shard = P("expert", "replica", None)
    return jax.shard_map(
        per_device,
        mesh=mesh,
        in_specs=(tok,) * 4 + (full,) * 3 + (shard,) * 3,
        out_specs=(tok, tok, shard, shard, shard),
        check_vma=False,
    )
```

profile of v0, /device:TPU:0, one launch (start us, length us, event | category | flops | bytes accessed | tf_op | source)
XLA Modules:
  0.0 101.9 jit_solution(9843671237118331061)
XLA Ops:
  0.6 0.1 pad_add_fusion.where
  0.7 0.0 copy-start.14
  0.7 0.7 copy-done.14
  1.4 0.7 copy-done.16
  2.1 0.9 copy-done.24
  3.0 0.9 copy-done.26
  3.9 2.3 %shard_map.137 = (bf16[8,56,1024]{2,1,0:T(8,128)(2,1)}, f32[2,16,128]{2,1,0:T(8,128)S(1)}, f32[2,8,128]{2,1,0:T(8,128)S(1)}) custom-call(s32[2]{0:T(128)S(1)} %pad_add_fusion.where, s32[6,64]{1,0:T(8,128)S(1)} %bitcast.8, bf16[6,64]{1,0:T(8,128)(2,1)S(1)} %bitcast.10, bf16[64,1024]{1,0:T(8,128)(2,1)S(1)} %copy-done.24, bf16[64,1024]{1,0:T(8,128)(2,1)S(1)} %copy-done.26), custom_call_target="tpu_custom_call" | custom-call | flops 117440512 | bytes 1206528 | tf_op jit(solution)/shard_map/pallas_call | solution.py:24
  6.2 0.0 copy-start.12
  6.2 0.6 copy-done.12
  6.8 6.2 %all-to-all-start = ((bf16[8,56,1024]{2,1,0:T(8,128)(2,1)}), bf16[8,56,1024]{2,1,0:T(8,128)(2,1)S(1)}, u32[]{:S(2)}, u32[]{:S(2)}) async-start(bf16[8,56,1024]{2,1,0:T(8,128)(2,1)} %get-tuple-element.28), calls=%async_computation | async-start | bytes 1835008 | tf_op jit(solution)/shard_map/all_to_all | solution.py:318
  13.0 0.0 copy-done.25
  13.0 2.7 %collective-permute-start.1 = (bf16[64,1024]{1,0:T(8,128)(2,1)S(1)}, bf16[64,1024]{1,0:T(8,128)(2,1)S(1)}, u32[]{:S(2)}, u32[]{:S(2)}) collective-permute-start(bf16[64,1024]{1,0:T(8,128)(2,1)S(1)} %copy-done.25), channel_id=1, source_target_pairs={{0,16},{2,18},{4,20},{6,22},{8,24},{10,26},{12,28},{14,30},{16,0},... | collective-permute-start | bytes 393224 | tf_op jit(solution)/shard_map/ppermute | solution.py:313
  15.6 0.0 copy-done.27
  15.6 0.3 collective-permute-start.2
  16.0 2.6 %collective-permute-start = (f32[2,8,128]{2,1,0:T(8,128)S(1)}, f32[2,8,128]{2,1,0:T(8,128)S(1)}, u32[]{:S(2)}, u32[]{:S(2)}) collective-permute-start(f32[2,8,128]{2,1,0:T(8,128)S(1)} %get-tuple-element.30), channel_id=1, source_target_pairs={{0,16},{2,18},{4,20},{6,22},{8,24},{10,26},{12,28},{14,30},{16,0},... | collective-permute-start | bytes 24584 | tf_op jit(solution)/shard_map/ppermute | solution.py:313
  18.6 10.2 %collective-permute-done.far = f32[2,8,128]{2,1,0:T(8,128)S(1)} collective-permute-done((f32[2,8,128]{2,1,0:T(8,128)S(1)}, f32[2,8,128]{2,1,0:T(8,128)S(1)}, u32[]{:S(2)}, u32[]{:S(2)}) %collective-permute-start) | collective-permute-done | bytes 8224 | tf_op jit(solution)/shard_map/ppermute | solution.py:313
  28.8 0.0 collective-permute-done.1.tok
  28.8 0.0 collective-permute-done.2.grad
  28.8 1.7 %shard_map.139 = bf16[8,56,1024]{2,1,0:T(8,128)(2,1)} custom-call(s32[2]{0:T(128)S(1)} %pad_add_fusion.where, f32[2,8,128]{2,1,0:T(8,128)S(1)} %collective-permute-done.far, bf16[64,1024]{1,0:T(8,128)(2,1)S(1)} %collective-permute-done.1.tok, bf16[64,1024]{1,0:T(8,128)(2,1)S(1)} %collective-permute-done.2.grad), custom_call_target="tpu_custom_call" | custom-call | flops 117440512 | bytes 1187840 | tf_op jit(solution)/shard_map/pallas_call | solution.py:24
  30.5 0.9 all-to-all-done.got
  31.4 7.1 %all-to-all-start.2 = ((bf16[8,56,1024]{2,1,0:T(8,128)(2,1)}), bf16[8,56,1024]{2,1,0:T(8,128)(2,1)S(1)}, u32[]{:S(2)}, u32[]{:S(2)}) async-start(bf16[8,56,1024]{2,1,0:T(8,128)(2,1)} %shard_map.139), calls=%async_computation.2 | async-start | bytes 1835008 | tf_op jit(solution)/shard_map/all_to_all | solution.py:318
  38.4 1.1 %copy-done.18 = bf16[1,1024,384]{2,1,0:T(8,128)(2,1)S(1)} copy-done((bf16[1,1024,384]{2,1,0:T(8,128)(2,1)S(1)}, bf16[1,1024,384]{2,1,0:T(8,128)(2,1)}, u32[]{:S(2)}) %copy-start.18) | copy-done | bytes 786456
  39.6 1.1 %copy-done.20 = bf16[1,1024,384]{2,1,0:T(8,128)(2,1)S(1)} copy-done((bf16[1,1024,384]{2,1,0:T(8,128)(2,1)S(1)}, bf16[1,1024,384]{2,1,0:T(8,128)(2,1)}, u32[]{:S(2)}) %copy-start.20) | copy-done | bytes 786456
  40.7 1.1 %copy-done.22 = bf16[1,1024,384]{2,1,0:T(8,128)(2,1)S(1)} copy-done((bf16[1,1024,384]{2,1,0:T(8,128)(2,1)S(1)}, bf16[1,1024,384]{2,1,0:T(8,128)(2,1)}, u32[]{:S(2)}) %copy-start.22) | copy-done | bytes 786456
  41.8 3.7 %shard_map.138 = (bf16[8,56,512]{2,1,0:T(8,128)(2,1)S(1)}, bf16[256,1024]{1,0:T(8,128)(2,1)S(1)}, bf16[256,1024]{1,0:T(8,128)(2,1)S(1)}, bf16[256,768]{1,0:T(8,1...) custom-call(s32[2]{0:T(128)S(1)} %pad_add_fusion.where, bf16[8,56,1024]{2,1,0:T(8,128)(2,1)S(1)} %all-to-all-done.got, ...), custom_call_target="tpu_custom_call" | custom-call | flops 1006632960 | bytes 5378048 | tf_op jit(solution)/shard_map/pallas_call | solution.py:24
  45.5 0.0 copy-start.5
  45.5 0.8 copy-done.5
  46.3 0.7 copy-done.8
  47.0 3.6 %all-to-all-done.2.got = bf16[8,56,1024]{2,1,0:T(8,128)(2,1)S(1)} async-done(((bf16[8,56,1024]{2,1,0:T(8,128)(2,1)}), bf16[8,56,1024]{2,1,0:T(8,128)(2,1)S(1)}, u32[]{:S(2)}, u32[]{:S(2)}) %all-to-all-start.2) | async-done | bytes 917536 | tf_op jit(solution)/shard_map/all_to_all | solution.py:318
  50.5 1.1 %copy-done.19 = bf16[1,1024,384]{2,1,0:T(8,128)(2,1)S(1)} copy-done((bf16[1,1024,384]{2,1,0:T(8,128)(2,1)S(1)}, bf16[1,1024,384]{2,1,0:T(8,128)(2,1)}, u32[]{:S(2)}) %copy-start.19) | copy-done | bytes 786456
  51.7 1.1 %copy-done.21 = bf16[1,1024,384]{2,1,0:T(8,128)(2,1)S(1)} copy-done((bf16[1,1024,384]{2,1,0:T(8,128)(2,1)S(1)}, bf16[1,1024,384]{2,1,0:T(8,128)(2,1)}, u32[]{:S(2)}) %copy-start.21) | copy-done | bytes 786456
  52.8 1.1 %copy-done.23 = bf16[1,1024,384]{2,1,0:T(8,128)(2,1)S(1)} copy-done((bf16[1,1024,384]{2,1,0:T(8,128)(2,1)S(1)}, bf16[1,1024,384]{2,1,0:T(8,128)(2,1)}, u32[]{:S(2)}) %copy-start.23) | copy-done | bytes 786456
  53.9 3.6 %shard_map.140 = (bf16[8,56,512]{2,1,0:T(8,128)(2,1)}, bf16[256,1024]{1,0:T(8,128)(2,1)S(1)}, bf16[256,1024]{1,0:T(8,128)(2,1)S(1)}, bf16[256,768]{1,0:T(8,128)(...) custom-call(s32[2]{0:T(128)S(1)} %pad_add_fusion.where, bf16[8,56,1024]{2,1,0:T(8,128)(2,1)S(1)} %all-to-all-done.2.got, ...), custom_call_target="tpu_custom_call" | custom-call | flops 1006632960 | bytes 5378048 | tf_op jit(solution)/shard_map/pallas_call | solution.py:24
  57.5 0.0 copy-start.3
  57.6 0.8 copy-done.3
  58.3 0.7 copy-done.6
  59.1 0.7 copy-done.10
  59.8 10.5 %all_to_all.25.sums = f32[16,8,128]{2,1,0:T(8,128)S(1)} all-to-all(f32[16,8,128]{2,1,0:T(8,128)S(1)} %broadcast_in_dim.2), channel_id=1, replica_groups=mesh['expert'=16,'replica'=2] {'expert'}, dimensions={0} | all-to-all | bytes 131072 | tf_op jit(solution)/shard_map/all_to_all | solution.py:417
  70.3 3.5 %all-to-all-start.3 = ((bf16[8,56,512]{2,1,0:T(8,128)(2,1)}), bf16[8,56,512]{2,1,0:T(8,128)(2,1)S(1)}, u32[]{:S(2)}, u32[]{:S(2)}) async-start(bf16[8,56,512]{2,1,0:T(8,128)(2,1)} %get-tuple-element.31), calls=%async_computation.3 | async-start | bytes 917504 | tf_op jit(solution)/shard_map/all_to_all | solution.py:318
  73.8 0.0 copy-done.9
  73.8 0.0 copy-start.4
  73.8 0.0 copy-start.7
  73.8 0.0 copy-start.11
  73.8 1.5 %shard_map.143.part = f32[2,512,1152]{2,1,0:T(8,128)S(1)} custom-call(s32[2]{0:T(128)S(1)} %pad_add_fusion.where, bf16[256,1024]{1,0:T(8,128)(2,1)S(1)} %get-tuple-element.40.first, bf16[256,1024]{1,0:T(8,128)(2,1)S(1)} %get-tuple-element.41.second, bf16[256,768]{1,0:T(8,128)(2,1)S(1)} %get-tuple-element.42.small, bf16[256,384]{1,0:T(8,128)(2,1)S(1)} %copy-done.9), custom_call_target="tpu_custom_call" | custom-call | flops 603979776 | bytes 6356992 | tf_op jit(solution)/shard_map/pallas_call | solution.py:24
  75.3 0.0 copy-done.4
  75.3 0.0 copy-done.7
  75.3 0.0 copy-done.11
  75.3 2.5 %shard_map.144 = (bf16[512,1152]{1,0:T(8,128)(2,1)S(1)}, bf16[512,1152]{1,0:T(8,128)(2,1)}) custom-call(s32[2]{0:T(128)S(1)} %pad_add_fusion.where, bf16[256,1024]{1,0:T(8,128)(2,1)S(1)} %get-tuple-element.36.first, bf16[256,1024]{1,0:T(8,128)(2,1)S(1)} %copy-done.4, bf16[256,768]{1,0:T(8,128)(2,1)S(1)} %copy-done.7, bf16[256,384]{1,0:T(8,128)(2,1)S(1)} %copy-done.11, ...), custom_call_target="tpu_custom_call" | custom-call | flops 603979776 | bytes 8716288 | tf_op jit(solution)/shard_map/pallas_call | solution.py:24
  77.8 0.0 collective-permute-start.4
  77.8 3.3 %all-to-all-done.3.returned = bf16[8,56,512]{2,1,0:T(8,128)(2,1)S(1)} async-done(((bf16[8,56,512]{2,1,0:T(8,128)(2,1)}), bf16[8,56,512]{2,1,0:T(8,128)(2,1)S(1)}, u32[]{:S(2)}, u32[]{:S(2)}) %all-to-all-start.3) | async-done | bytes 458784 | tf_op jit(solution)/shard_map/all_to_all | solution.py:318
  81.1 3.5 %all-to-all-start.1 = ((bf16[8,56,512]{2,1,0:T(8,128)(2,1)}), bf16[8,56,512]{2,1,0:T(8,128)(2,1)S(1)}, u32[]{:S(2)}, u32[]{:S(2)}) async-start(bf16[8,56,512]{2,1,0:T(8,128)(2,1)} %copy-done.5), calls=%async_computation.1 | async-start | bytes 917504 | tf_op jit(solution)/shard_map/all_to_all | solution.py:318
  84.6 0.8 shard_map.141
  85.4 0.8 collective-permute-start.3
  86.2 8.5 %all-to-all-done.1.returned = bf16[8,56,512]{2,1,0:T(8,128)(2,1)S(1)} async-done(((bf16[8,56,512]{2,1,0:T(8,128)(2,1)}), bf16[8,56,512]{2,1,0:T(8,128)(2,1)S(1)}, u32[]{:S(2)}, u32[]{:S(2)}) %all-to-all-start.1) | async-done | bytes 458784 | tf_op jit(solution)/shard_map/all_to_all | solution.py:318
  94.7 0.0 collective-permute-done.3.partial
  94.7 0.0 copy-done.13
  94.7 0.0 copy-done.15
  94.7 0.0 copy-done.17
  94.8 1.8 %shard_map.142 = (bf16[64,1024]{1,0:T(8,128)(2,1)}, bf16[6,64]{1,0:T(8,128)(2,1)}) custom-call(s32[2]{0:T(128)S(1)} %pad_add_fusion.where, f32[2,16,128]{2,1,0:T(8,128)S(1)} %copy-done.13, bf16[8,56,512]{2,1,0:T(8,128)(2,1)S(1)} %all-to-all-done.1.returned, bf16[64,1024]{1,0:T(8,128)(2,1)S(1)} %collective-permute-done.3.partial, ...), custom_call_target="tpu_custom_call" | custom-call | flops 58720256 | bytes 805888 | tf_op jit(solution)/shard_map/pallas_call | solution.py:24
  96.6 0.0 collective-permute-done.4.refs_1_
  96.6 1.1 %copy-done = f32[1,512,384]{2,1,0:T(8,128)S(1)} copy-done((f32[1,512,384]{2,1,0:T(8,128)S(1)}, f32[1,512,384]{2,1,0:T(8,128)}, u32[]{:S(2)}) %copy-start) | copy-done | bytes 786456
  97.7 1.1 %copy-done.1 = f32[1,512,384]{2,1,0:T(8,128)S(1)} copy-done((f32[1,512,384]{2,1,0:T(8,128)S(1)}, f32[1,512,384]{2,1,0:T(8,128)}, u32[]{:S(2)}) %copy-start.1) | copy-done | bytes 786456
  98.8 1.1 %copy-done.2 = f32[1,512,384]{2,1,0:T(8,128)S(1)} copy-done((f32[1,512,384]{2,1,0:T(8,128)S(1)}, f32[1,512,384]{2,1,0:T(8,128)}, u32[]{:S(2)}) %copy-start.2) | copy-done | bytes 786456
  100.0 1.9 %update.1 = (f32[1,512,384]{2,1,0:T(8,128)}, f32[1,512,384]{2,1,0:T(8,128)}, f32[1,512,384]{2,1,0:T(8,128)}) custom-call(bf16[512,1152]{1,0:T(8,128)(2,1)S(1)} %get-tuple-element.44.refs_0_, bf16[512,1152]{1,0:T(8,128)(2,1)S(1)} %collective-permute-done.4.refs_1_, f32[1,512,384]{2,1,0:T(8,128)S(1)} %copy-done, f32[1,512,384]{2,1,0:T(8,128)S(1)} %copy-done.1, ...), custom_call_target="tpu_custom_call" | custom-call | flops 1769472 | bytes 7077888 | tf_op jit(solution)/shard_map/update/pallas_call | solution.py:421
  (23 shorter events, 0.0 us)
Async XLA Ops:
  0.7 0.7 copy-start.14
  1.4 0.7 copy-start.16
  2.1 0.9 copy-start.24
  3.0 0.9 copy-start.26
  3.9 9.1 %copy-start.25 = (bf16[64,1024]{1,0:T(8,128)(2,1)S(1)}, bf16[64,1024]{1,0:T(8,128)(2,1)}, u32[]{:S(2)}) copy-start(bf16[64,1024]{1,0:T(8,128)(2,1)} %tok.1) | copy-start | bytes 393220
  3.9 11.7 %copy-start.27 = (bf16[64,1024]{1,0:T(8,128)(2,1)S(1)}, bf16[64,1024]{1,0:T(8,128)(2,1)}, u32[]{:S(2)}) copy-start(bf16[64,1024]{1,0:T(8,128)(2,1)} %grad.1) | copy-start | bytes 393220
  6.2 0.6 copy-start.12
  6.8 24.6 %all-to-all-start = ((bf16[8,56,1024]{2,1,0:T(8,128)(2,1)}), bf16[8,56,1024]{2,1,0:T(8,128)(2,1)S(1)}, u32[]{:S(2)}, u32[]{:S(2)}) async-start(bf16[8,56,1024]{2,1,0:T(8,128)(2,1)} %get-tuple-element.28), calls=%async_computation | async-start | bytes 1835008 | tf_op jit(solution)/shard_map/all_to_all | solution.py:318
  13.0 15.8 %collective-permute-start.1 = (bf16[64,1024]{1,0:T(8,128)(2,1)S(1)}, bf16[64,1024]{1,0:T(8,128)(2,1)S(1)}, u32[]{:S(2)}, u32[]{:S(2)}) collective-permute-start(bf16[64,1024]{1,0:T(8,128)(2,1)S(1)} %copy-done.25), channel_id=1, source_target_pairs={{0,16},{2,18},{4,20},{6,22},{8,24},{10,26},{12,28},{14,30},{16,0},... | collective-permute-start | bytes 393224 | tf_op jit(solution)/shard_map/ppermute | solution.py:313
  15.6 13.1 %collective-permute-start.2 = (bf16[64,1024]{1,0:T(8,128)(2,1)S(1)}, bf16[64,1024]{1,0:T(8,128)(2,1)S(1)}, u32[]{:S(2)}, u32[]{:S(2)}) collective-permute-start(bf16[64,1024]{1,0:T(8,128)(2,1)S(1)} %copy-done.27), channel_id=1, source_target_pairs={{0,16},{2,18},{4,20},{6,22},{8,24},{10,26},{12,28},{14,30},{16,0},... | collective-permute-start | bytes 393224 | tf_op jit(solution)/shard_map/ppermute | solution.py:313
  16.0 12.8 %collective-permute-start = (f32[2,8,128]{2,1,0:T(8,128)S(1)}, f32[2,8,128]{2,1,0:T(8,128)S(1)}, u32[]{:S(2)}, u32[]{:S(2)}) collective-permute-start(f32[2,8,128]{2,1,0:T(8,128)S(1)} %get-tuple-element.30), channel_id=1, source_target_pairs={{0,16},{2,18},{4,20},{6,22},{8,24},{10,26},{12,28},{14,30},{16,0},... | collective-permute-start | bytes 24584 | tf_op jit(solution)/shard_map/ppermute | solution.py:313
  31.4 19.1 %all-to-all-start.2 = ((bf16[8,56,1024]{2,1,0:T(8,128)(2,1)}), bf16[8,56,1024]{2,1,0:T(8,128)(2,1)S(1)}, u32[]{:S(2)}, u32[]{:S(2)}) async-start(bf16[8,56,1024]{2,1,0:T(8,128)(2,1)} %shard_map.139), calls=%async_computation.2 | async-start | bytes 1835008 | tf_op jit(solution)/shard_map/all_to_all | solution.py:318
  38.4 1.1 %copy-start.18 = (bf16[1,1024,384]{2,1,0:T(8,128)(2,1)S(1)}, bf16[1,1024,384]{2,1,0:T(8,128)(2,1)}, u32[]{:S(2)}) copy-start(bf16[1,1024,384]{2,1,0:T(8,128)(2,1)} %param.14) | copy-start | bytes 2359300
  39.6 1.1 %copy-start.20 = (bf16[1,1024,384]{2,1,0:T(8,128)(2,1)S(1)}, bf16[1,1024,384]{2,1,0:T(8,128)(2,1)}, u32[]{:S(2)}) copy-start(bf16[1,1024,384]{2,1,0:T(8,128)(2,1)} %param.15) | copy-start | bytes 2359300
  40.7 1.1 %copy-start.22 = (bf16[1,1024,384]{2,1,0:T(8,128)(2,1)S(1)}, bf16[1,1024,384]{2,1,0:T(8,128)(2,1)}, u32[]{:S(2)}) copy-start(bf16[1,1024,384]{2,1,0:T(8,128)(2,1)} %param.16) | copy-start | bytes 2359300
  45.5 0.8 copy-start.5
  46.3 0.7 copy-start.8
  50.5 1.1 %copy-start.19 = (bf16[1,1024,384]{2,1,0:T(8,128)(2,1)S(1)}, bf16[1,1024,384]{2,1,0:T(8,128)(2,1)}, u32[]{:S(2)}) copy-start(bf16[1,1024,384]{2,1,0:T(8,128)(2,1)} %param.14) | copy-start | bytes 2359300
  51.7 1.1 %copy-start.21 = (bf16[1,1024,384]{2,1,0:T(8,128)(2,1)S(1)}, bf16[1,1024,384]{2,1,0:T(8,128)(2,1)}, u32[]{:S(2)}) copy-start(bf16[1,1024,384]{2,1,0:T(8,128)(2,1)} %param.15) | copy-start | bytes 2359300
  52.8 1.1 %copy-start.23 = (bf16[1,1024,384]{2,1,0:T(8,128)(2,1)S(1)}, bf16[1,1024,384]{2,1,0:T(8,128)(2,1)}, u32[]{:S(2)}) copy-start(bf16[1,1024,384]{2,1,0:T(8,128)(2,1)} %param.16) | copy-start | bytes 2359300
  57.5 0.8 copy-start.3
  58.3 0.7 copy-start.6
  59.1 0.7 copy-start.10
  59.8 14.0 %copy-start.9 = (bf16[256,384]{1,0:T(8,128)(2,1)S(1)}, bf16[256,384]{1,0:T(8,128)(2,1)}, u32[]{:S(2)}) copy-start(bf16[256,384]{1,0:T(8,128)(2,1)} %copy-done.8) | copy-start | bytes 589828
  70.3 10.8 %all-to-all-start.3 = ((bf16[8,56,512]{2,1,0:T(8,128)(2,1)}), bf16[8,56,512]{2,1,0:T(8,128)(2,1)S(1)}, u32[]{:S(2)}, u32[]{:S(2)}) async-start(bf16[8,56,512]{2,1,0:T(8,128)(2,1)} %get-tuple-element.31), calls=%async_computation.3 | async-start | bytes 917504 | tf_op jit(solution)/shard_map/all_to_all | solution.py:318
  73.8 1.5 %copy-start.4 = (bf16[256,1024]{1,0:T(8,128)(2,1)S(1)}, bf16[256,1024]{1,0:T(8,128)(2,1)}, u32[]{:S(2)}) copy-start(bf16[256,1024]{1,0:T(8,128)(2,1)} %copy-done.3) | copy-start | bytes 1572868
  73.8 1.5 %copy-start.7 = (bf16[256,768]{1,0:T(8,128)(2,1)S(1)}, bf16[256,768]{1,0:T(8,128)(2,1)}, u32[]{:S(2)}) copy-start(bf16[256,768]{1,0:T(8,128)(2,1)} %copy-done.6) | copy-start | bytes 1179652
  73.8 1.5 %copy-start.11 = (bf16[256,384]{1,0:T(8,128)(2,1)S(1)}, bf16[256,384]{1,0:T(8,128)(2,1)}, u32[]{:S(2)}) copy-start(bf16[256,384]{1,0:T(8,128)(2,1)} %copy-done.10) | copy-start | bytes 589828
  77.8 17.0 %copy-start.13 = (f32[2,16,128]{2,1,0:T(8,128)S(1)}, f32[2,16,128]{2,1,0:T(8,128)}, u32[]{:S(2)}) copy-start(f32[2,16,128]{2,1,0:T(8,128)} %copy-done.12) | copy-start | bytes 49156
  77.8 17.0 %copy-start.15 = (s32[64,6]{0,1:T(8,128)S(1)}, s32[64,6]{0,1:T(8,128)}, u32[]{:S(2)}) copy-start(s32[64,6]{0,1:T(8,128)} %param.11) | copy-start | bytes 4612
  77.8 17.0 %copy-start.17 = (bf16[64,6]{0,1:T(8,128)(2,1)S(1)}, bf16[64,6]{0,1:T(8,128)(2,1)}, u32[]{:S(2)}) copy-start(bf16[64,6]{0,1:T(8,128)(2,1)} %param.12) | copy-start | bytes 2308
  77.8 18.8 %collective-permute-start.4 = (bf16[512,1152]{1,0:T(8,128)(2,1)}, bf16[512,1152]{1,0:T(8,128)(2,1)S(1)}, u32[]{:S(2)}, u32[]{:S(2)}) collective-permute-start(bf16[512,1152]{1,0:T(8,128)(2,1)} %get-tuple-element.45), channel_id=1, source_target_pairs={{0,1},{1,0},{2,3},{3,2},{4,5},{5,4},{6,7},{7,6},{8,9},{9,8},{10,11... | collective-permute-start | bytes 3538952 | tf_op jit(solution)/shard_map/ppermute | solution.py:398
  81.1 13.6 %all-to-all-start.1 = ((bf16[8,56,512]{2,1,0:T(8,128)(2,1)}), bf16[8,56,512]{2,1,0:T(8,128)(2,1)S(1)}, u32[]{:S(2)}, u32[]{:S(2)}) async-start(bf16[8,56,512]{2,1,0:T(8,128)(2,1)} %copy-done.5), calls=%async_computation.1 | async-start | bytes 917504 | tf_op jit(solution)/shard_map/all_to_all | solution.py:318
  85.4 9.3 %collective-permute-start.3 = (bf16[64,1024]{1,0:T(8,128)(2,1)S(1)}, bf16[64,1024]{1,0:T(8,128)(2,1)S(1)}, u32[]{:S(2)}, u32[]{:S(2)}) collective-permute-start(bf16[64,1024]{1,0:T(8,128)(2,1)S(1)} %shard_map.141), channel_id=1, source_target_pairs={{0,16},{2,18},{4,20},{6,22},{8,24},{10,26},{12,28},{14,30},{16,0},... | collective-permute-start | bytes 393224 | tf_op jit(solution)/shard_map/ppermute | solution.py:313
  96.6 1.1 %copy-start = (f32[1,512,384]{2,1,0:T(8,128)S(1)}, f32[1,512,384]{2,1,0:T(8,128)}, u32[]{:S(2)}) copy-start(f32[1,512,384]{2,1,0:T(8,128)} %refs_2_.1) | copy-start | bytes 2359300
  97.7 1.1 %copy-start.1 = (f32[1,512,384]{2,1,0:T(8,128)S(1)}, f32[1,512,384]{2,1,0:T(8,128)}, u32[]{:S(2)}) copy-start(f32[1,512,384]{2,1,0:T(8,128)} %refs_3_.1) | copy-start | bytes 2359300
  98.8 1.1 %copy-start.2 = (f32[1,512,384]{2,1,0:T(8,128)S(1)}, f32[1,512,384]{2,1,0:T(8,128)}, u32[]{:S(2)}) copy-start(f32[1,512,384]{2,1,0:T(8,128)} %refs_4_.1) | copy-start | bytes 2359300
where the time goes:
time: 103 us; the launch traced here: 102 us
  starting transfers between devices  26.6 us (26%)
  waiting for transfers between devices  26.5 us (26%)
  Pallas kernels  19.7 us (19%)
  local copies, waits for them, and re-layouts  17.7 us (17%)
  blocking collectives  10.5 us (10%)
    all_to_all x4, starting transfers between devices, within(): lax.all_to_all(x, 'expert', split_axis=0, concat_axis=0, tiled=True, axis...  20.2 us
    pallas_call x8, Pallas kernels, call(): pl.pallas_call(kernel, out_shape=tuple(outs), in_specs=[SMEM] + [ANY if i...  17.8 us
    unnamed x56, local copies, waits for them, and re-layouts  17.7 us
    all_to_all x4, waiting for transfers between devices, within(): lax.all_to_all(x, 'expert', split_axis=0, concat_axis=0, tiled=True, axis...  16.3 us
    all_to_all x1, blocking collectives, per_device(): lax.all_to_all(sums, 'expert', split_axis=0, concat_axis=0, tiled=True)  10.5 us
    ppermute x4, waiting for transfers between devices, across(): lax.ppermute(x, 'expert', [(i, (i + sub) % experts) for i in range(expert...  10.2 us
    ppermute x4, starting transfers between devices, across(): lax.ppermute(x, 'expert', [(i, (i + sub) % experts) for i in range(expert...  6.38 us
  transfers between devices with their start and end apart: 9, of which 5 were waited for; matrix products, arithmetic and copies ran while one was open for 0% of the time, Pallas kernels for 12%

commit v1 on v0

v1 whole, which is shorter than its diff:
```python
import functools

import jax
import jax.numpy as jnp
from jax import lax
from jax.experimental import pallas as pl
from jax.experimental.pallas import tpu as pltpu
from jax.sharding import PartitionSpec as P


F32 = jnp.float32
BF16 = jnp.bfloat16
ROWS_BY_ROWS = (((0,), (0,)), ((), ()))
COLS_BY_COLS = (((1,), (1,)), ((), ()))
VMEM = pl.BlockSpec(memory_space=pltpu.VMEM)
SMEM = pl.BlockSpec(memory_space=pltpu.SMEM)


HBM = pl.BlockSpec(memory_space=pltpu.HBM)


def call(kernel, outs, ins, flops, scratch=(), streamed=(), out_streamed=(), limit=16):
    nbytes = sum(x.size * x.dtype.itemsize for x in list(ins[1:]) + list(outs))
    ins = [
        pltpu.with_memory_space_constraint(x, pltpu.HBM) if i in streamed else x
        for i, x in enumerate(ins)
    ]
    outs = [
        pltpu.HBM(x.shape, x.dtype) if i in out_streamed else x for i, x in enumerate(outs)
    ]
    return pl.pallas_call(
        kernel,
        out_shape=tuple(outs),
        in_specs=[SMEM] + [HBM if i in streamed else VMEM for i in range(1, len(ins))],
        out_specs=tuple(HBM if i in out_streamed else VMEM for i in range(len(outs))),
        scratch_shapes=list(scratch),
        cost_estimate=pl.CostEstimate(flops=flops, bytes_accessed=nbytes, transcendentals=0),
        compiler_params=pltpu.CompilerParams(vmem_limit_bytes=limit << 20),
    )(*ins)


class Layout:
    def __init__(self, cap):
        self.cap = cap
        self.whole = cap // 8 * 8
        self.rest = cap - self.whole
        self.mixed = -(-2 * self.rest // 8) * 8
        self.rows = 2 * self.whole + self.mixed
        self.side = self.whole + self.mixed

    def row(self, slot, second):
        late = slot >= self.whole
        first_row = slot + jnp.where(late, 1.0 * self.whole, 0.0)
        second_row = slot + jnp.where(late, 1.0 * (self.whole + self.rest), 1.0 * self.whole)
        return jnp.where(second, second_row, first_row)


def selection(key, value, chunk):
    experts, lanes = key.shape
    slot = lax.broadcasted_iota(jnp.int32, (experts, chunk, lanes), 1)
    hit = slot == key.astype(jnp.int32)[:, None, :]
    full = jnp.where(hit, jnp.broadcast_to(value[:, None, :], hit.shape), 0.0)
    return full.reshape(experts * chunk, lanes).astype(BF16)


def pack(pairs, both, chunk, staged, outs, sems):
    copies = []
    for e, (key, value) in enumerate(pairs):
        pick = selection(key, value, chunk)
        staged[e] = jnp.dot(pick, both, preferred_element_type=F32).astype(BF16)
        copies.append(pltpu.make_async_copy(staged.at[e], outs[e], sems.at[e]))
        copies[-1].start()
    for copy in copies:
        copy.wait()


def route_kernel(lay, sub, where, ids_in, weights_in, tok, grad, *refs):
    packed, (table, far, ids, weights, both, staged, in_sems, sems) = refs[:sub], refs[sub:]
    rows = tok.shape[0]
    loads = [
        pltpu.make_async_copy(ids_in, ids, in_sems.at[0]),
        pltpu.make_async_copy(weights_in, weights, in_sems.at[1]),
        pltpu.make_async_copy(tok, both.at[pl.ds(0, rows)], in_sems.at[2]),
        pltpu.make_async_copy(grad, both.at[pl.ds(rows, rows)], in_sems.at[3]),
    ]
    for load in loads:
        load.start()
    topk = ids.shape[0]
    experts, lanes = table.shape[1], table.shape[2]
    source = lax.broadcasted_iota(jnp.int32, (rows, lanes), 0)
    lane = lax.broadcasted_iota(jnp.int32, (rows, lanes), 1)
    target = jnp.where(lane >= rows, lane - rows, lane)
    earlier = jnp.where(source < target, 1.0, 0.0).astype(BF16)
    same = jnp.where(source == target, 1.0, 0.0).astype(BF16)
    expert = lax.broadcasted_iota(jnp.int32, (experts, rows), 0)
    named = jnp.zeros((experts, rows), F32)
    weight = jnp.zeros((experts, rows), F32)
    loads[0].wait()
    loads[1].wait()
    for k in range(topk):
        hit = ids[k : k + 1, :] == expert
        named = named + jnp.where(hit, 1.0, 0.0)
        weight = weight + jnp.where(hit, weights[k : k + 1, :].astype(F32), 0.0)
    named_b = named.astype(BF16)
    position = jnp.dot(named_b, earlier, preferred_element_type=F32)
    present = jnp.dot(named_b, same, preferred_element_type=F32)
    factor = jnp.dot(weight.astype(BF16), same, preferred_element_type=F32)
    second = lax.broadcasted_iota(jnp.int32, (experts, lanes), 1) >= rows
    table[0] = jnp.where(present > 0.5, lay.row(position, second), -1.0)
    table[1] = jnp.where(second, factor, 1.0)
    other = pl.ds(pl.multiple_of((1 - where[0]) * sub, sub), sub)
    far[0] = table[0, other, :]
    far[1] = table[1, other, :]
    loads[2].wait()
    loads[3].wait()
    pairs = []
    for offset in range(sub):
        row = pl.ds(where[0] * sub + (where[2] ^ offset), 1)
        pairs.append((table[0, row, :], table[1, row, :]))
    pack(pairs, both[...], lay.rows, staged, packed, sems)


def relay_kernel(lay, where, far, tok, grad, packed, staged, sems):
    both = jnp.concatenate([tok[...], grad[...]], axis=0)
    sub = packed.shape[0]
    pairs = [(far[0, e : e + 1], far[1, e : e + 1]) for e in range(sub)]
    pack(pairs, both, lay.rows, staged, [packed.at[e] for e in range(sub)], sems)


def split_sides(lay, got, first, second):
    for e, chunk in enumerate(got):
        at, side, whole = e * lay.side, lay.side, lay.whole
        if whole:
            first[at : at + whole] = chunk[:whole]
            second[at : at + whole] = chunk[whole : 2 * whole]
        first[at + whole : at + side] = chunk[2 * whole :]
        second[at + whole : at + side] = chunk[2 * whole :]


def align(lay, x, experts):
    parts = []
    for e in range(experts):
        at = e * lay.side
        if lay.whole:
            parts.append(x[at : at + lay.whole])
        late = x[at + lay.whole : at + lay.side]
        parts.append(pltpu.roll(late, lay.mixed - lay.rest, 0) if lay.rest else late)
    return jnp.concatenate(parts, axis=0)


def expert_kernel(lay, sub, direct, where, *refs):
    if direct:
        got, refs = refs[:sub], refs[sub:]
    else:
        got, refs = [refs[0].at[e] for e in range(sub)], refs[1:]
    gate_in, up_in, down_in, back_rows, *kept = refs[:8]
    w_gate, w_up, w_down, staged, first, second, small, down_small = refs[8:16]
    in_sems, sems, kept_sems = refs[16:19]
    loads = [
        pltpu.make_async_copy(gate_in, w_gate, in_sems.at[0]),
        pltpu.make_async_copy(up_in, w_up, in_sems.at[1]),
        pltpu.make_async_copy(down_in, w_down, in_sems.at[2]),
    ]
    stores = [
        pltpu.make_async_copy(held, out, kept_sems.at[i])
        for i, (held, out) in enumerate(zip((first, second, small, down_small), kept))
    ]
    width, units = w_gate.shape
    total = sub * lay.side
    if direct:
        local, local_sems = refs[19:]
        arrivals = [
            pltpu.make_async_copy(got[e], local.at[e], local_sems.at[e]) for e in range(sub)
        ]
        for copy in arrivals + loads:
            copy.start()
        for copy in arrivals:
            copy.wait()
        got = [local.at[e] for e in range(sub)]
    else:
        for load in loads:
            load.start()
    split_sides(lay, got, first, second)
    stores[0].start()
    stores[1].start()
    loads[0].wait()
    gate = jnp.dot(first[...], w_gate[...], preferred_element_type=F32)
    loads[1].wait()
    up = jnp.dot(first[...], w_up[...], preferred_element_type=F32)
    loads[2].wait()
    back = jnp.dot(second[...], w_down[...], preferred_element_type=F32)
    back = align(lay, back, sub)
    slot = lax.broadcasted_iota(jnp.int32, (sub, lay.side, 128), 1).reshape(total, 128)
    filled = slot[:, :1] < lay.cap
    sig = 1.0 / (1.0 + jnp.exp(-gate))
    act = gate * sig
    hidden = jnp.where(filled, act * up, 0.0)
    grad_gate = jnp.where(filled, back * up * sig * (1.0 + gate * (1.0 - sig)), 0.0).astype(BF16)
    grad_up = jnp.where(filled, back * act, 0.0).astype(BF16)
    slot_grad = lax.dot_general(grad_gate, w_gate[...], COLS_BY_COLS, preferred_element_type=F32)
    slot_grad = slot_grad + lax.dot_general(
        grad_up, w_up[...], COLS_BY_COLS, preferred_element_type=F32
    )
    route = jnp.sum(hidden * back, axis=1, keepdims=True)
    lane = lax.broadcasted_iota(jnp.int32, (total, 128), 1)
    spread = jnp.where(lane == slot, route, 0.0).reshape(sub, lay.side, 128)
    sums = jnp.sum(spread, axis=1)
    half = width // 2
    copies = []
    early = lax.broadcasted_iota(jnp.int32, (lay.mixed, half), 0) < lay.rest
    for e in range(sub):
        at, whole = e * lay.side, lay.whole
        if whole:
            staged[e, :whole] = slot_grad[at : at + whole, :half].astype(BF16)
            staged[e, whole : 2 * whole] = slot_grad[at : at + whole, half:].astype(BF16)
        late = slot_grad[at + whole : at + lay.side]
        if lay.rest:
            mixed = jnp.where(early, late[:, :half], pltpu.roll(late[:, half:], lay.rest, 0))
            staged[e, 2 * whole : lay.rows] = mixed.astype(BF16)
        staged[e, lay.rows :, :128] = jnp.broadcast_to(sums[e : e + 1], (8, 128)).astype(BF16)
        staged[e, lay.rows :, 128:] = jnp.zeros((8, half - 128), BF16)
        target = (where[2] ^ e) if direct else e
        copies.append(pltpu.make_async_copy(staged.at[e], back_rows.at[target], sems.at[e]))
        copies[-1].start()
    small[:, :units] = grad_gate
    small[:, units:] = grad_up
    stores[2].start()
    parts = []
    for e in range(sub):
        at, whole = e * lay.side, lay.whole
        if whole:
            parts.append(hidden[at : at + whole])
        late = hidden[at + whole : at + lay.side]
        parts.append(pltpu.roll(late, lay.rest, 0) if lay.rest else late)
    down_small[...] = jnp.concatenate(parts, axis=0).astype(BF16)
    stores[3].start()
    for copy in copies + stores:
        copy.wait()


def weight_kernel(replicas, where, *refs):
    sources, outs, refs = refs[:8], refs[8 : 8 + replicas], refs[8 + replicas :]
    held, (firsts, seconds, sems) = refs[:4], refs[4:]
    first, second, small, down_small = held
    width = firsts.shape[2]
    units = down_small.shape[1]
    total = sources[0].shape[0]
    loads = []
    for i in range(8):
        rows = pl.ds((i // 4) * total, total)
        loads.append(pltpu.make_async_copy(sources[i], held[i % 4].at[rows], sems.at[i]))
        loads[-1].start()
    for load in loads:
        load.wait()
    for b in range(replicas):
        cols = slice(b * width, (b + 1) * width)
        firsts[b] = first[:, cols]
        seconds[b] = second[:, cols]
    for s in reversed(range(replicas)):
        b = lax.rem(where[1] + s, replicas)
        outs[s][:, : 2 * units] = lax.dot_general(
            firsts[b], small[...], ROWS_BY_ROWS, preferred_element_type=F32
        ).astype(BF16)
        outs[s][:, 2 * units :] = lax.dot_general(
            seconds[b], down_small[...], ROWS_BY_ROWS, preferred_element_type=F32
        ).astype(BF16)


def update_kernel(replicas, where, *refs):
    parts, moms, outs = refs[:replicas], refs[replicas : replicas + 3], refs[replicas + 3 :]
    outs, (held, made, in_sems, out_sems) = outs[:3], outs[3:]
    units = moms[0].shape[2]
    loads = [pltpu.make_async_copy(moms[i].at[0], held.at[i], in_sems.at[i]) for i in range(3)]
    stores = [pltpu.make_async_copy(made.at[i], outs[i].at[0], out_sems.at[i]) for i in range(3)]
    for load in loads:
        load.start()
    for i in range(3):
        cols = slice(i * units, (i + 1) * units)
        total = parts[0][:, cols].astype(F32)
        for part in parts[1:]:
            total = total + part[:, cols].astype(F32)
        loads[i].wait()
        made[i] = 0.9 * held[i] + 0.1 * total
        stores[i].start()
    for store in stores:
        store.wait()


def gathered(key, returned):
    ones = jnp.ones(key.shape, F32)
    chunk = returned.shape[1]
    flat = returned.reshape(returned.shape[0] * chunk, returned.shape[2])
    return lax.dot_general(
        selection(key, ones, chunk), flat, ROWS_BY_ROWS, preferred_element_type=F32
    )


def route_values(lay, key, returned):
    key = jnp.where(key >= lay.whole, key - lay.whole, key).astype(jnp.int32)
    value = jnp.zeros(key.shape, F32)
    per_slot = returned[:, lay.rows, :128].astype(F32)
    for q in range(lay.cap):
        value = value + jnp.where(key == q, per_slot[:, q : q + 1], 0.0)
    return value


def partial_kernel(lay, rows, where, far, returned, out):
    sub, _, half = returned.shape
    lanes = far.shape[2]
    total = gathered(far[0], returned[...])
    out[:rows, :half] = total[:rows].astype(BF16)
    out[:rows, half:] = total[rows:].astype(BF16)
    out[rows:, :lanes] = route_values(lay, far[0], returned[...]).astype(BF16)
    out[rows:, lanes:] = jnp.zeros((sub, 2 * half - lanes), BF16)


def final_kernel(lay, where, table, returned, partial, ids, weights, out, route):
    rows, half = out.shape[0], returned.shape[2]
    topk = ids.shape[0]
    sub = returned.shape[0]
    own = table[0, pl.ds(pl.multiple_of(where[0] * sub, sub), sub), :]
    total = gathered(own, returned[...])
    out[:, :half] = (total[:rows] + partial[:rows, :half].astype(F32)).astype(BF16)
    out[:, half:] = (total[rows:] + partial[:rows, half:].astype(F32)).astype(BF16)
    near = route_values(lay, own, returned[...])[:, :rows]
    far = partial[rows:, :rows].astype(F32)
    expert = lax.broadcasted_iota(jnp.int32, (sub, rows), 0)
    near_expert, far_expert = expert + where[0] * sub, expert + (1 - where[0]) * sub
    for k in range(topk):
        name = ids[k : k + 1, :]
        picked = jnp.where(name == near_expert, near, 0.0)
        picked = picked + jnp.where(name == far_expert, far, 0.0)
        picked = jnp.sum(picked, axis=0, keepdims=True)
        route[k : k + 1, :] = (picked / weights[k : k + 1, :].astype(F32)).astype(BF16)


def per_device(
    tokens, route_ids, route_weights, out_grad, w_gate, w_up, w_down, mom_gate, mom_up, mom_down
):
    experts = lax.axis_size("expert")
    replicas = lax.axis_size("replica")
    rows, width = tokens.shape
    topk = route_ids.shape[1]
    units = w_gate.shape[2]
    lay = Layout(7 * rows * topk // (6 * experts))
    sub = experts // 2
    lanes = 2 * rows
    half = width // 2
    strip = width // replicas
    total = sub * lay.side
    me = lax.axis_index("expert")
    place = me // sub
    where = jnp.stack([place, lax.axis_index("replica"), me % sub]).astype(jnp.int32)
    groups = [list(range(sub)), list(range(sub, experts))]
    S = jax.ShapeDtypeStruct
    DMA = pltpu.SemaphoreType.DMA

    def permute(x, partner):
        return lax.ppermute(x, "expert", [(i, partner(i)) for i in range(experts)])

    def across(x):
        return permute(x, lambda i: (i + sub) % experts)

    def within(x):
        return lax.all_to_all(
            x, "expert", split_axis=0, concat_axis=0, tiled=True, axis_index_groups=groups
        )

    ids = route_ids.T
    weights = route_weights.T
    far_tok = across(tokens)
    far_grad = across(out_grad)
    chunk = S((lay.rows, width), BF16)
    staged = pltpu.VMEM((sub, *chunk.shape), BF16)
    *packed, table, far = call(
        functools.partial(route_kernel, lay, sub),
        [chunk] * sub + [S((2, experts, lanes), F32), S((2, sub, lanes), F32)],
        (where, ids, weights, tokens, out_grad),
        2 * sub * lay.rows * lanes * width,
        scratch=[
            pltpu.VMEM(ids.shape, ids.dtype),
            pltpu.VMEM(weights.shape, weights.dtype),
            pltpu.VMEM((2 * rows, width), BF16),
            staged,
            DMA((4,)),
            DMA((sub,)),
        ],
        streamed=(1, 2, 3, 4),
        out_streamed=range(sub),
    )
    far = across(far)
    got_a = packed[:1] + [permute(packed[offset], lambda i: i ^ offset) for offset in range(1, sub)]
    (relayed,) = call(
        functools.partial(relay_kernel, lay),
        [S((sub, *chunk.shape), BF16)],
        (where, far, far_tok, far_grad),
        2 * sub * lay.rows * lanes * width,
        scratch=[staged, DMA((sub,))],
        out_streamed=(0,),
    )
    got_b = [within(relayed)]

    def expert(got, direct):
        weight = pltpu.VMEM((width, units), BF16)
        back = S((sub, lay.rows + 8, half), BF16)
        kept = [S((total, cols), BF16) for cols in (width, width, 2 * units, units)]
        local = [pltpu.VMEM((sub, *chunk.shape), BF16), DMA((sub,))]
        first_weight = len(got) + 1
        return call(
            functools.partial(expert_kernel, lay, sub, direct),
            [back] + kept,
            (where, *got, w_gate[0], w_up[0], w_down[0]),
            10 * total * width * units,
            scratch=[weight, weight, weight, pltpu.VMEM(back.shape, BF16)]
            + [pltpu.VMEM(x.shape, BF16) for x in kept]
            + [DMA((3,)), DMA((sub,)), DMA((4,))]
            + (local if direct else []),
            streamed=range(1 if direct else first_weight, first_weight + 3),
            out_streamed=range(5),
        )

    back_a, *factors_a = expert(got_a, True)
    back_b, *factors_b = expert(got_b, False)
    ret_b = within(back_b)
    turned = pltpu.VMEM((replicas, 2 * total, strip), BF16)
    parts = call(
        functools.partial(weight_kernel, replicas),
        [S((strip, 3 * units), BF16)] * replicas,
        (where, *factors_a, *factors_b),
        12 * total * width * units,
        scratch=[pltpu.VMEM((2 * x.shape[0], x.shape[1]), BF16) for x in factors_a]
        + [turned, turned, DMA((8,))],
        streamed=range(1, 9),
        limit=16 if strip >= 128 else 48,
    )
    moved = [
        lax.ppermute(
            parts[s], "replica", [(i, (i + s) % replicas) for i in range(replicas)]
        )
        for s in range(1, replicas)
    ]
    (partial,) = call(
        functools.partial(partial_kernel, lay, rows),
        [S((rows + sub, width), BF16)],
        (where, far, ret_b),
        2 * sub * lay.rows * lanes * half,
    )
    partial = across(partial)
    ret_a = within(back_a)
    new = call(
        functools.partial(update_kernel, replicas),
        [S(mom_gate.shape, F32)] * 3,
        (where, parts[0], *moved, mom_gate, mom_up, mom_down),
        9 * strip * units,
        scratch=[pltpu.VMEM((3, strip, units), F32)] * 2 + [DMA((3,)), DMA((3,))],
        streamed=range(replicas + 1, replicas + 4),
        out_streamed=range(3),
    )
    grad_tokens, grad_route = call(
        functools.partial(final_kernel, lay),
        [S((rows, width), BF16), S((topk, rows), BF16)],
        (where, table, ret_a, partial, ids, weights),
        2 * sub * lay.rows * lanes * half,
    )
    return (grad_tokens, grad_route.T, *new)


def solution(mesh):
    tok = P(("expert", "replica"), None)
    full = P("expert", None, None)
    shard = P("expert", "replica", None)
    return jax.shard_map(
        per_device,
        mesh=mesh,
        in_specs=(tok,) * 4 + (full,) * 3 + (shard,) * 3,
        out_specs=(tok, tok, shard, shard, shard),
        check_vma=False,
    )
```

time: 103 us -> 103 us (level)
  local copies, waits for them, and re-layouts: 17.7 us -> 5.93 us
  blocking collectives: 10.5 us -> 17.9 us
  Pallas kernels: 19.7 us -> 25.1 us
  waiting for transfers between devices: 26.5 us -> 24.6 us
  starting transfers between devices: 26.6 us -> 28.1 us
    ppermute x4 -> x11, starting transfers between devices: 6.38 us -> 21 us  [permute(): return lax.ppermute(x, 'expert', [(i, partner(i)) for i in range(experts)])]
    all_to_all x4 -> x2, starting transfers between devices: 20.2 us -> 7.01 us  [within(): lax.all_to_all(x, 'expert', split_axis=0, concat_axis=0, tiled=True, axis...]
    unnamed x56 -> x46, local copies, waits for them, and re-layouts: 17.7 us -> 5.93 us
    all_to_all x4 -> x2, waiting for transfers between devices: 16.3 us -> 7.23 us  [within(): lax.all_to_all(x, 'expert', split_axis=0, concat_axis=0, tiled=True, axis...]
    all_to_all x1, blocking collectives: 10.5 us -> 17.9 us  [within(): lax.all_to_all(x, 'expert', split_axis=0, concat_axis=0, tiled=True, axis...]
    ppermute x4 -> x11, waiting for transfers between devices: 10.2 us -> 17.4 us  [permute(): return lax.ppermute(x, 'expert', [(i, partner(i)) for i in range(experts)])]
    pallas_call x9 -> x8, Pallas kernels: 19.7 us -> 25.1 us  [call(): pl.pallas_call(kernel, out_shape=tuple(outs), in_specs=[SMEM] + [HBM if i...]
  transfers between devices with their start and end apart: 9 -> 14, of which waited for: 5 -> 5; matrix products, arithmetic and copies ran while one was open for 0% -> 0% of each run, Pallas kernels for 12% -> 15%
where the time goes in v1:
time: 103 us
  starting transfers between devices  28.1 us (27%)
  Pallas kernels  25.1 us (24%)
  waiting for transfers between devices  24.6 us (24%)
  blocking collectives  17.9 us (17%)
  local copies, waits for them, and re-layouts  5.93 us (6%)
    pallas_call x8, Pallas kernels, call(): pl.pallas_call(kernel, out_shape=tuple(outs), in_specs=[SMEM] + [HBM if i...  25.1 us
    ppermute x11, starting transfers between devices, permute(): return lax.ppermute(x, 'expert', [(i, partner(i)) for i in range(experts)])  21 us
    all_to_all x1, blocking collectives, within(): lax.all_to_all(x, 'expert', split_axis=0, concat_axis=0, tiled=True, axis...  17.9 us
    ppermute x11, waiting for transfers between devices, permute(): return lax.ppermute(x, 'expert', [(i, partner(i)) for i in range(experts)])  17.4 us
    all_to_all x2, waiting for transfers between devices, within(): lax.all_to_all(x, 'expert', split_axis=0, concat_axis=0, tiled=True, axis...  7.23 us
    all_to_all x2, starting transfers between devices, within(): lax.all_to_all(x, 'expert', split_axis=0, concat_axis=0, tiled=True, axis...  7.01 us
    unnamed x46, local copies, waits for them, and re-layouts  5.93 us
  transfers between devices with their start and end apart: 14, of which 5 were waited for; matrix products, arithmetic and copies ran while one was open for 0% of the time, Pallas kernels for 15%

profile of v1, /device:TPU:0, one launch (start us, length us, event | category | flops | bytes accessed | tf_op | source)
XLA Modules:
  0.0 102.6 jit_solution(16493389325703804163)
XLA Ops:
  0.6 4.1 %collective-permute-start.8 = (bf16[64,1024]{1,0:T(8,128)(2,1)}, bf16[64,1024]{1,0:T(8,128)(2,1)S(1)}, u32[]{:S(2)}, u32[]{:S(2)}) collective-permute-start(bf16[64,1024]{1,0:T(8,128)(2,1)} %tok.1), channel_id=1, source_target_pairs={{0,16},{2,18},{4,20},{6,22},{8,24},{10,26},{12,28},{14,30},{16,0},... | collective-permute-start | bytes 393224 | tf_op jit(solution)/shard_map/ppermute | solution.py:359
  4.8 0.1 collective-permute-start.9
  4.8 0.1 pad_add_fusion.where
  4.9 2.7 %shard_map.137 = (bf16[56,1024]{1,0:T(8,128)(2,1)}, bf16[56,1024]{1,0:T(8,128)(2,1)}, bf16[56,1024]{1,0:T(8,128)(2,1)}, bf16[56,1024]{1,0:T(8,128)(2,1)}, bf16[5...) custom-call(s32[3]{0:T(128)S(1)} %pad_add_fusion.where, ...), custom_call_target="tpu_custom_call" | custom-call | flops 117440512 | bytes 1206528 | tf_op jit(solution)/shard_map/pallas_call | solution.py:31
  7.7 0.0 copy-start.2
  7.7 0.6 copy-done.2
  8.3 2.8 %collective-permute-start.7 = (f32[2,8,128]{2,1,0:T(8,128)S(1)}, f32[2,8,128]{2,1,0:T(8,128)S(1)}, u32[]{:S(2)}, u32[]{:S(2)}) collective-permute-start(f32[2,8,128]{2,1,0:T(8,128)S(1)} %get-tuple-element.42), channel_id=1, source_target_pairs={{0,16},{2,18},{4,20},{6,22},{8,24},{10,26},{12,28},{14,30},{16,0},... | collective-permute-start | bytes 24584 | tf_op jit(solution)/shard_map/ppermute | solution.py:359
  11.1 6.1 %collective-permute-done.7.far = f32[2,8,128]{2,1,0:T(8,128)S(1)} collective-permute-done((f32[2,8,128]{2,1,0:T(8,128)S(1)}, f32[2,8,128]{2,1,0:T(8,128)S(1)}, u32[]{:S(2)}, u32[]{:S(2)}) %collective-permute-start.7) | collective-permute-done | bytes 8224 | tf_op jit(solution)/shard_map/ppermute | solution.py:359
  17.2 0.0 collective-permute-done.8.tok
  17.3 0.0 collective-permute-done.9.grad
  17.3 1.7 %shard_map.139 = bf16[8,56,1024]{2,1,0:T(8,128)(2,1)} custom-call(s32[3]{0:T(128)S(1)} %pad_add_fusion.where, f32[2,8,128]{2,1,0:T(8,128)S(1)} %collective-permute-done.7.far, bf16[64,1024]{1,0:T(8,128)(2,1)S(1)} %collective-permute-done.8.tok, bf16[64,1024]{1,0:T(8,128)(2,1)S(1)} %collective-permute-done.9.grad), custom_call_target="tpu_custom_call" | custom-call | flops 117440512 | bytes 1187840 | tf_op jit(solution)/shard_map/pallas_call | solution.py:31
  19.0 0.0 copy-start
  19.0 0.6 copy-done
  19.6 17.9 %all_to_all.15.refs_0_ = bf16[8,56,1024]{2,1,0:T(8,128)(2,1)S(1)} all-to-all(bf16[8,56,1024]{2,1,0:T(8,128)(2,1)} %shard_map.139), channel_id=1, replica_groups={{0,2,4,6,8,10,12,14},{16,18,20,22,24,26,28,30},{1,3,5,7,9,11,13,15},{17..., dimensions={0} | all-to-all | bytes 1835008 | tf_op jit(solution)/shard_map/all_to_all | solution.py:365
  37.5 0.0 copy-start.11
  37.5 0.0 copy-start.10
  37.5 0.0 copy-start.9
  37.5 5.0 %shard_map.140 = (bf16[8,64,512]{2,1,0:T(8,128)(2,1)}, bf16[256,1024]{1,0:T(8,128)(2,1)}, bf16[256,1024]{1,0:T(8,128)(2,1)}, bf16[256,768]{1,0:T(8,128)(2,1)}, bf16[256,384]{1,0:T(8,128)(2,1)}) custom-call(s32[3]{0:T(128)S(1)} %pad_add_fusion.where, bf16[8,56,1024]{2,1,0:T(8,128)(2,1)S(1)} %all_to_all.15.refs_0_, bf16[1024,384]{1,0:T(8,128)(2,1)} %bitcast.13, ...), custom_call_target="tpu_custom_call" | custom-call | flops 1006632960 | bytes 5439488 | tf_op jit(solution)/shard_map/pallas_call | solution.py:31
  42.5 3.5 %all-to-all-start.2 = ((bf16[8,64,512]{2,1,0:T(8,128)(2,1)}), bf16[8,64,512]{2,1,0:T(8,128)(2,1)S(1)}, u32[]{:S(2)}, u32[]{:S(2)}) async-start(bf16[8,64,512]{2,1,0:T(8,128)(2,1)} %get-tuple-element.43), calls=%async_computation.2 | async-start | bytes 1048576 | tf_op jit(solution)/shard_map/all_to_all | solution.py:365
  46.1 0.0 copy-done.15
  46.1 1.9 %collective-permute-start = (bf16[56,1024]{1,0:T(8,128)(2,1)S(1)}, bf16[56,1024]{1,0:T(8,128)(2,1)S(1)}, u32[]{:S(2)}, u32[]{:S(2)}) collective-permute-start(bf16[56,1024]{1,0:T(8,128)(2,1)S(1)} %copy-done.15), channel_id=1, source_target_pairs={{0,2},{2,0},{4,6},{6,4},{8,10},{10,8},{12,14},{14,12},{16,18},{18,... | collective-permute-start | bytes 344072 | tf_op jit(solution)/shard_map/ppermute | solution.py:359
  48.0 0.0 copy-done.14
  48.0 1.5 %collective-permute-start.1 = (bf16[56,1024]{1,0:T(8,128)(2,1)S(1)}, bf16[56,1024]{1,0:T(8,128)(2,1)S(1)}, u32[]{:S(2)}, u32[]{:S(2)}) collective-permute-start(bf16[56,1024]{1,0:T(8,128)(2,1)S(1)} %copy-done.14), channel_id=1, source_target_pairs={{0,4},{2,6},{4,0},{6,2},{8,12},{10,14},{12,8},{14,10},{16,20},{18,... | collective-permute-start | bytes 344072 | tf_op jit(solution)/shard_map/ppermute | solution.py:359
  49.5 0.0 copy-done.13
  49.5 0.2 collective-permute-start.2
  49.6 0.0 copy-done.12
  49.6 1.9 %collective-permute-start.3 = (bf16[56,1024]{1,0:T(8,128)(2,1)S(1)}, bf16[56,1024]{1,0:T(8,128)(2,1)S(1)}, u32[]{:S(2)}, u32[]{:S(2)}) collective-permute-start(bf16[56,1024]{1,0:T(8,128)(2,1)S(1)} %copy-done.12), channel_id=1, source_target_pairs={{0,8},{2,10},{4,12},{6,14},{8,0},{10,2},{12,4},{14,6},{16,24},{18,... | collective-permute-start | bytes 344072 | tf_op jit(solution)/shard_map/ppermute | solution.py:359
  51.5 0.0 copy-done.11
  51.5 1.4 %collective-permute-start.4 = (bf16[56,1024]{1,0:T(8,128)(2,1)S(1)}, bf16[56,1024]{1,0:T(8,128)(2,1)S(1)}, u32[]{:S(2)}, u32[]{:S(2)}) collective-permute-start(bf16[56,1024]{1,0:T(8,128)(2,1)S(1)} %copy-done.11), channel_id=1, source_target_pairs={{0,10},{2,8},{4,14},{6,12},{8,2},{10,0},{12,6},{14,4},{16,26},{18,... | collective-permute-start | bytes 344072 | tf_op jit(solution)/shard_map/ppermute | solution.py:359
  52.9 4.7 %collective-permute-done.refs_1_ = bf16[56,1024]{1,0:T(8,128)(2,1)S(1)} collective-permute-done((bf16[56,1024]{1,0:T(8,128)(2,1)S(1)}, bf16[56,1024]{1,0:T(8,128)(2,1)S(1)}, u32[]{:S(2)}, u32[]{:S(2)}) %collective-permute-start) | collective-permute-done | bytes 114720 | tf_op jit(solution)/shard_map/ppermute | solution.py:359
  57.7 0.0 copy-done.10
  57.7 3.6 %collective-permute-start.5 = (bf16[56,1024]{1,0:T(8,128)(2,1)S(1)}, bf16[56,1024]{1,0:T(8,128)(2,1)S(1)}, u32[]{:S(2)}, u32[]{:S(2)}) collective-permute-start(bf16[56,1024]{1,0:T(8,128)(2,1)S(1)} %copy-done.10), channel_id=1, source_target_pairs={{0,12},{2,14},{4,8},{6,10},{8,4},{10,6},{12,0},{14,2},{16,28},{18,... | collective-permute-start | bytes 344072 | tf_op jit(solution)/shard_map/ppermute | solution.py:359
  61.2 0.0 collective-permute-done.1.refs_2_
  61.2 0.0 copy-done.9
  61.2 0.1 collective-permute-start.6
  61.3 0.0 collective-permute-done.2.refs_3_
  61.3 0.0 collective-permute-done.3.refs_4_
  61.4 0.0 collective-permute-done.4.refs_5_
  61.4 0.0 copy-start.20
  61.4 2.7 %collective-permute-done.5.refs_6_ = bf16[56,1024]{1,0:T(8,128)(2,1)S(1)} collective-permute-done((bf16[56,1024]{1,0:T(8,128)(2,1)S(1)}, bf16[56,1024]{1,0:T(8,128)(2,1)S(1)}, u32[]{:S(2)}, u32[]{:S(2)}) %collective-permute-start.5) | collective-permute-done | bytes 114720 | tf_op jit(solution)/shard_map/ppermute | solution.py:359
  64.1 3.8 %collective-permute-done.6.refs_7_ = bf16[56,1024]{1,0:T(8,128)(2,1)S(1)} collective-permute-done((bf16[56,1024]{1,0:T(8,128)(2,1)S(1)}, bf16[56,1024]{1,0:T(8,128)(2,1)S(1)}, u32[]{:S(2)}, u32[]{:S(2)}) %collective-permute-start.6) | collective-permute-done | bytes 114720 | tf_op jit(solution)/shard_map/ppermute | solution.py:359
  67.9 0.0 copy-done.17
  67.9 0.0 copy-done.19
  67.9 0.0 copy-done.20
  67.9 0.0 copy-done.21
  67.9 0.6 copy-done.22
  68.5 5.3 %shard_map.138 = (bf16[8,64,512]{2,1,0:T(8,128)(2,1)}, bf16[256,1024]{1,0:T(8,128)(2,1)}, bf16[256,1024]{1,0:T(8,128)(2,1)}, bf16[256,768]{1,0:T(8,128)(2,1)}, bf16[256,384]{1,0:T(8,128)(2,1)}) custom-call(s32[3]{0:T(128)S(1)} %pad_add_fusion.where, bf16[56,1024]{1,0:T(8,128)(2,1)} %get-tuple-element.33.refs_0_, bf16[56,1024]{1,0:T(8,128)(2,1)} %copy-done.16, ...), custom_call_target="tpu_custom_call" | custom-call | flops 1006632960 | bytes 5439488 | tf_op jit(solution)/shard_map/pallas_call | solution.py:31
  73.9 4.7 %shard_map.143 = (bf16[512,1152]{1,0:T(8,128)(2,1)S(1)}, bf16[512,1152]{1,0:T(8,128)(2,1)}) custom-call(s32[3]{0:T(128)S(1)} %pad_add_fusion.where, bf16[256,1024]{1,0:T(8,128)(2,1)} %get-tuple-element.46.refs_0_, bf16[256,1024]{1,0:T(8,128)(2,1)} %get-tuple-element.47.refs_1_, bf16[256,768]{1,0:T(8,128)(2,1)} %get-tuple-element.48.refs_2_, ...), custom_call_target="tpu_custom_call" | custom-call | flops 1207959552 | bytes 5636096 | tf_op jit(solution)/shard_map/pallas_call | solution.py:31
  78.5 0.1 collective-permute-start.11
  78.6 0.0 all-to-all-done.2.returned
  78.6 3.5 %all-to-all-start = ((bf16[8,64,512]{2,1,0:T(8,128)(2,1)}), bf16[8,64,512]{2,1,0:T(8,128)(2,1)S(1)}, u32[]{:S(2)}, u32[]{:S(2)}) async-start(bf16[8,64,512]{2,1,0:T(8,128)(2,1)} %get-tuple-element.41), calls=%async_computation | async-start | bytes 1048576 | tf_op jit(solution)/shard_map/all_to_all | solution.py:365
  82.2 0.7 copy-done.1
  82.8 0.7 copy-done.5
  83.5 0.8 shard_map.141
  84.4 3.4 %collective-permute-start.10 = (bf16[72,1024]{1,0:T(8,128)(2,1)S(1)}, bf16[72,1024]{1,0:T(8,128)(2,1)S(1)}, u32[]{:S(2)}, u32[]{:S(2)}) collective-permute-start(bf16[72,1024]{1,0:T(8,128)(2,1)S(1)} %shard_map.141), channel_id=1, source_target_pairs={{0,16},{2,18},{4,20},{6,22},{8,24},{10,26},{12,28},{14,30},{16,0},... | collective-permute-start | bytes 442376 | tf_op jit(solution)/shard_map/ppermute | solution.py:359
  87.8 7.2 %all-to-all-done.returned = bf16[8,64,512]{2,1,0:T(8,128)(2,1)S(1)} async-done(((bf16[8,64,512]{2,1,0:T(8,128)(2,1)}), bf16[8,64,512]{2,1,0:T(8,128)(2,1)S(1)}, u32[]{:S(2)}, u32[]{:S(2)}) %all-to-all-start) | async-done | bytes 524320 | tf_op jit(solution)/shard_map/all_to_all | solution.py:365
  95.0 0.0 collective-permute-done.10.partial
  95.0 0.7 copy-done.3
  95.7 0.7 copy-done.6
  96.4 0.7 copy-done.7
  97.1 0.7 copy-done.8
  97.8 1.5 %shard_map.142 = (bf16[64,1024]{1,0:T(8,128)(2,1)}, bf16[6,64]{1,0:T(8,128)(2,1)}) custom-call(s32[3]{0:T(128)S(1)} %copy-done.6, f32[2,16,128]{2,1,0:T(8,128)S(1)} %copy-done.3, bf16[8,64,512]{2,1,0:T(8,128)(2,1)S(1)} %all-to-all-done.returned, bf16[72,1024]{1,0:T(8,128)(2,1)S(1)} %collective-permute-done.10.partial, s32[6,64]{1,0:T(8,128)S(1)} %bitcast.10, ...), custom_call_target="tpu_custom_call" | custom-call | flops 58720256 | bytes 822272 | tf_op jit(solution)/shard_map/pallas_call | solution.py:31
  99.2 0.0 collective-permute-done.11.refs_1_
  99.2 3.4 %shard_map.144 = (f32[1,512,384]{2,1,0:T(8,128)}, f32[1,512,384]{2,1,0:T(8,128)}, f32[1,512,384]{2,1,0:T(8,128)}) custom-call(s32[3]{0:T(128)S(1)} %copy-done.6, bf16[512,1152]{1,0:T(8,128)(2,1)S(1)} %get-tuple-element.54.refs_0_, bf16[512,1152]{1,0:T(8,128)(2,1)S(1)} %collective-permute-done.11.refs_1_, f32[1,512,384]{2,1,0:T(8,128)} %refs_2_.1, ...), custom_call_target="tpu_custom_call" | custom-call | flops 1769472 | bytes 7077888 | tf_op jit(solution)/shard_map/pallas_call | solution.py:31
  (20 shorter events, 0.0 us)
Async XLA Ops:
  0.6 16.6 %collective-permute-start.8 = (bf16[64,1024]{1,0:T(8,128)(2,1)}, bf16[64,1024]{1,0:T(8,128)(2,1)S(1)}, u32[]{:S(2)}, u32[]{:S(2)}) collective-permute-start(bf16[64,1024]{1,0:T(8,128)(2,1)} %tok.1), channel_id=1, source_target_pairs={{0,16},{2,18},{4,20},{6,22},{8,24},{10,26},{12,28},{14,30},{16,0},... | collective-permute-start | bytes 393224 | tf_op jit(solution)/shard_map/ppermute | solution.py:359
  4.8 12.5 %collective-permute-start.9 = (bf16[64,1024]{1,0:T(8,128)(2,1)}, bf16[64,1024]{1,0:T(8,128)(2,1)S(1)}, u32[]{:S(2)}, u32[]{:S(2)}) collective-permute-start(bf16[64,1024]{1,0:T(8,128)(2,1)} %grad.1), channel_id=1, source_target_pairs={{0,16},{2,18},{4,20},{6,22},{8,24},{10,26},{12,28},{14,30},{16,0},... | collective-permute-start | bytes 393224 | tf_op jit(solution)/shard_map/ppermute | solution.py:359
  4.9 68.9 %copy-start.4 = (s32[3]{0:T(128)}, s32[3]{0:T(128)S(1)}, u32[]{:S(2)}) copy-start(s32[3]{0:T(128)S(1)} %pad_add_fusion.where) | copy-start | bytes 40
  7.7 0.6 copy-start.2
  8.3 9.0 %collective-permute-start.7 = (f32[2,8,128]{2,1,0:T(8,128)S(1)}, f32[2,8,128]{2,1,0:T(8,128)S(1)}, u32[]{:S(2)}, u32[]{:S(2)}) collective-permute-start(f32[2,8,128]{2,1,0:T(8,128)S(1)} %get-tuple-element.42), channel_id=1, source_target_pairs={{0,16},{2,18},{4,20},{6,22},{8,24},{10,26},{12,28},{14,30},{16,0},... | collective-permute-start | bytes 24584 | tf_op jit(solution)/shard_map/ppermute | solution.py:359
  19.0 0.6 copy-start
  37.5 8.6 %copy-start.15 = (bf16[56,1024]{1,0:T(8,128)(2,1)S(1)}, bf16[56,1024]{1,0:T(8,128)(2,1)}, u32[]{:S(2)}) copy-start(bf16[56,1024]{1,0:T(8,128)(2,1)} %get-tuple-element.34) | copy-start | bytes 344068
  37.5 10.5 %copy-start.14 = (bf16[56,1024]{1,0:T(8,128)(2,1)S(1)}, bf16[56,1024]{1,0:T(8,128)(2,1)}, u32[]{:S(2)}) copy-start(bf16[56,1024]{1,0:T(8,128)(2,1)} %get-tuple-element.35) | copy-start | bytes 344068
  37.5 12.0 %copy-start.13 = (bf16[56,1024]{1,0:T(8,128)(2,1)S(1)}, bf16[56,1024]{1,0:T(8,128)(2,1)}, u32[]{:S(2)}) copy-start(bf16[56,1024]{1,0:T(8,128)(2,1)} %get-tuple-element.36) | copy-start | bytes 344068
  37.5 12.1 %copy-start.12 = (bf16[56,1024]{1,0:T(8,128)(2,1)S(1)}, bf16[56,1024]{1,0:T(8,128)(2,1)}, u32[]{:S(2)}) copy-start(bf16[56,1024]{1,0:T(8,128)(2,1)} %get-tuple-element.37) | copy-start | bytes 344068
  37.5 14.0 %copy-start.11 = (bf16[56,1024]{1,0:T(8,128)(2,1)S(1)}, bf16[56,1024]{1,0:T(8,128)(2,1)}, u32[]{:S(2)}) copy-start(bf16[56,1024]{1,0:T(8,128)(2,1)} %get-tuple-element.38) | copy-start | bytes 344068
  37.5 20.2 %copy-start.10 = (bf16[56,1024]{1,0:T(8,128)(2,1)S(1)}, bf16[56,1024]{1,0:T(8,128)(2,1)}, u32[]{:S(2)}) copy-start(bf16[56,1024]{1,0:T(8,128)(2,1)} %get-tuple-element.39) | copy-start | bytes 344068
  37.5 23.7 %copy-start.9 = (bf16[56,1024]{1,0:T(8,128)(2,1)S(1)}, bf16[56,1024]{1,0:T(8,128)(2,1)}, u32[]{:S(2)}) copy-start(bf16[56,1024]{1,0:T(8,128)(2,1)} %get-tuple-element.40) | copy-start | bytes 344068
  42.5 36.1 %all-to-all-start.2 = ((bf16[8,64,512]{2,1,0:T(8,128)(2,1)}), bf16[8,64,512]{2,1,0:T(8,128)(2,1)S(1)}, u32[]{:S(2)}, u32[]{:S(2)}) async-start(bf16[8,64,512]{2,1,0:T(8,128)(2,1)} %get-tuple-element.43), calls=%async_computation.2 | async-start | bytes 1048576 | tf_op jit(solution)/shard_map/all_to_all | solution.py:365
  46.1 11.6 %collective-permute-start = (bf16[56,1024]{1,0:T(8,128)(2,1)S(1)}, bf16[56,1024]{1,0:T(8,128)(2,1)S(1)}, u32[]{:S(2)}, u32[]{:S(2)}) collective-permute-start(bf16[56,1024]{1,0:T(8,128)(2,1)S(1)} %copy-done.15), channel_id=1, source_target_pairs={{0,2},{2,0},{4,6},{6,4},{8,10},{10,8},{12,14},{14,12},{16,18},{18,... | collective-permute-start | bytes 344072 | tf_op jit(solution)/shard_map/ppermute | solution.py:359
  48.0 13.3 %collective-permute-start.1 = (bf16[56,1024]{1,0:T(8,128)(2,1)S(1)}, bf16[56,1024]{1,0:T(8,128)(2,1)S(1)}, u32[]{:S(2)}, u32[]{:S(2)}) collective-permute-start(bf16[56,1024]{1,0:T(8,128)(2,1)S(1)} %copy-done.14), channel_id=1, source_target_pairs={{0,4},{2,6},{4,0},{6,2},{8,12},{10,14},{12,8},{14,10},{16,20},{18,... | collective-permute-start | bytes 344072 | tf_op jit(solution)/shard_map/ppermute | solution.py:359
  49.5 11.9 %collective-permute-start.2 = (bf16[56,1024]{1,0:T(8,128)(2,1)S(1)}, bf16[56,1024]{1,0:T(8,128)(2,1)S(1)}, u32[]{:S(2)}, u32[]{:S(2)}) collective-permute-start(bf16[56,1024]{1,0:T(8,128)(2,1)S(1)} %copy-done.13), channel_id=1, source_target_pairs={{0,6},{2,4},{4,2},{6,0},{8,14},{10,12},{12,10},{14,8},{16,22},{18,... | collective-permute-start | bytes 344072 | tf_op jit(solution)/shard_map/ppermute | solution.py:359
  49.6 11.7 %collective-permute-start.3 = (bf16[56,1024]{1,0:T(8,128)(2,1)S(1)}, bf16[56,1024]{1,0:T(8,128)(2,1)S(1)}, u32[]{:S(2)}, u32[]{:S(2)}) collective-permute-start(bf16[56,1024]{1,0:T(8,128)(2,1)S(1)} %copy-done.12), channel_id=1, source_target_pairs={{0,8},{2,10},{4,12},{6,14},{8,0},{10,2},{12,4},{14,6},{16,24},{18,... | collective-permute-start | bytes 344072 | tf_op jit(solution)/shard_map/ppermute | solution.py:359
  51.5 9.9 %collective-permute-start.4 = (bf16[56,1024]{1,0:T(8,128)(2,1)S(1)}, bf16[56,1024]{1,0:T(8,128)(2,1)S(1)}, u32[]{:S(2)}, u32[]{:S(2)}) collective-permute-start(bf16[56,1024]{1,0:T(8,128)(2,1)S(1)} %copy-done.11), channel_id=1, source_target_pairs={{0,10},{2,8},{4,14},{6,12},{8,2},{10,0},{12,6},{14,4},{16,26},{18,... | collective-permute-start | bytes 344072 | tf_op jit(solution)/shard_map/ppermute | solution.py:359
  57.7 10.2 %copy-start.16 = (bf16[56,1024]{1,0:T(8,128)(2,1)}, bf16[56,1024]{1,0:T(8,128)(2,1)S(1)}, u32[]{:S(2)}) copy-start(bf16[56,1024]{1,0:T(8,128)(2,1)S(1)} %collective-permute-done.refs_1_) | copy-start | bytes 344068
  57.7 6.4 %collective-permute-start.5 = (bf16[56,1024]{1,0:T(8,128)(2,1)S(1)}, bf16[56,1024]{1,0:T(8,128)(2,1)S(1)}, u32[]{:S(2)}, u32[]{:S(2)}) collective-permute-start(bf16[56,1024]{1,0:T(8,128)(2,1)S(1)} %copy-done.10), channel_id=1, source_target_pairs={{0,12},{2,14},{4,8},{6,10},{8,4},{10,6},{12,0},{14,2},{16,28},{18,... | collective-permute-start | bytes 344072 | tf_op jit(solution)/shard_map/ppermute | solution.py:359
  61.2 6.7 %copy-start.17 = (bf16[56,1024]{1,0:T(8,128)(2,1)}, bf16[56,1024]{1,0:T(8,128)(2,1)S(1)}, u32[]{:S(2)}) copy-start(bf16[56,1024]{1,0:T(8,128)(2,1)S(1)} %collective-permute-done.1.refs_2_) | copy-start | bytes 344068
  61.2 6.7 %collective-permute-start.6 = (bf16[56,1024]{1,0:T(8,128)(2,1)S(1)}, bf16[56,1024]{1,0:T(8,128)(2,1)S(1)}, u32[]{:S(2)}, u32[]{:S(2)}) collective-permute-start(bf16[56,1024]{1,0:T(8,128)(2,1)S(1)} %copy-done.9), channel_id=1, source_target_pairs={{0,14},{2,12},{4,10},{6,8},{8,6},{10,4},{12,2},{14,0},{16,30},{18,... | collective-permute-start | bytes 344072 | tf_op jit(solution)/shard_map/ppermute | solution.py:359
  61.3 6.6 %copy-start.18 = (bf16[56,1024]{1,0:T(8,128)(2,1)}, bf16[56,1024]{1,0:T(8,128)(2,1)S(1)}, u32[]{:S(2)}) copy-start(bf16[56,1024]{1,0:T(8,128)(2,1)S(1)} %collective-permute-done.2.refs_3_) | copy-start | bytes 344068
  61.4 6.6 %copy-start.19 = (bf16[56,1024]{1,0:T(8,128)(2,1)}, bf16[56,1024]{1,0:T(8,128)(2,1)S(1)}, u32[]{:S(2)}) copy-start(bf16[56,1024]{1,0:T(8,128)(2,1)S(1)} %collective-permute-done.3.refs_4_) | copy-start | bytes 344068
  61.4 6.6 %copy-start.20 = (bf16[56,1024]{1,0:T(8,128)(2,1)}, bf16[56,1024]{1,0:T(8,128)(2,1)S(1)}, u32[]{:S(2)}) copy-start(bf16[56,1024]{1,0:T(8,128)(2,1)S(1)} %collective-permute-done.4.refs_5_) | copy-start | bytes 344068
  64.1 3.8 %copy-start.21 = (bf16[56,1024]{1,0:T(8,128)(2,1)}, bf16[56,1024]{1,0:T(8,128)(2,1)S(1)}, u32[]{:S(2)}) copy-start(bf16[56,1024]{1,0:T(8,128)(2,1)S(1)} %collective-permute-done.5.refs_6_) | copy-start | bytes 344068
  67.9 0.6 copy-start.22
  78.5 20.7 %collective-permute-start.11 = (bf16[512,1152]{1,0:T(8,128)(2,1)}, bf16[512,1152]{1,0:T(8,128)(2,1)S(1)}, u32[]{:S(2)}, u32[]{:S(2)}) collective-permute-start(bf16[512,1152]{1,0:T(8,128)(2,1)} %get-tuple-element.55), channel_id=1, source_target_pairs={{0,1},{1,0},{2,3},{3,2},{4,5},{5,4},{6,7},{7,6},{8,9},{9,8},{10,11... | collective-permute-start | bytes 3538952 | tf_op jit(solution)/shard_map/ppermute | solution.py:437
  78.6 16.4 %all-to-all-start = ((bf16[8,64,512]{2,1,0:T(8,128)(2,1)}), bf16[8,64,512]{2,1,0:T(8,128)(2,1)S(1)}, u32[]{:S(2)}, u32[]{:S(2)}) async-start(bf16[8,64,512]{2,1,0:T(8,128)(2,1)} %get-tuple-element.41), calls=%async_computation | async-start | bytes 1048576 | tf_op jit(solution)/shard_map/all_to_all | solution.py:365
  82.1 0.7 copy-start.1
  82.8 0.7 copy-start.5
  84.4 10.7 %collective-permute-start.10 = (bf16[72,1024]{1,0:T(8,128)(2,1)S(1)}, bf16[72,1024]{1,0:T(8,128)(2,1)S(1)}, u32[]{:S(2)}, u32[]{:S(2)}) collective-permute-start(bf16[72,1024]{1,0:T(8,128)(2,1)S(1)} %shard_map.141), channel_id=1, source_target_pairs={{0,16},{2,18},{4,20},{6,22},{8,24},{10,26},{12,28},{14,30},{16,0},... | collective-permute-start | bytes 442376 | tf_op jit(solution)/shard_map/ppermute | solution.py:359
  95.0 0.7 copy-start.3
  95.7 0.7 copy-start.6
  96.4 0.7 copy-start.7
  97.1 0.7 copy-start.8

commit v2 on v1

--- a/solution.py
+++ b/solution.py
@@ -63,20 +63,26 @@
     return full.reshape(experts * chunk, lanes).astype(BF16)
 
 
-def pack(pairs, both, chunk, staged, outs, sems):
+def pack(keys, values, both, chunk, staged, outs, sems):
     copies = []
-    for e, (key, value) in enumerate(pairs):
-        pick = selection(key, value, chunk)
-        staged[e] = jnp.dot(pick, both, preferred_element_type=F32).astype(BF16)
-        copies.append(pltpu.make_async_copy(staged.at[e], outs[e], sems.at[e]))
-        copies[-1].start()
+    count = keys.shape[0]
+    group = max(1, count // 2)
+    for start in range(0, count, group):
+        here = slice(start, start + group)
+        pick = selection(keys[here], values[here], chunk)
+        made = jnp.dot(pick, both, preferred_element_type=F32)
+        staged[here] = made.reshape(group, chunk, -1).astype(BF16)
+        for e in range(start, start + group):
+            copies.append(pltpu.make_async_copy(staged.at[e], outs[e], sems.at[e]))
+            copies[-1].start()
     for copy in copies:
         copy.wait()
 
 
 def route_kernel(lay, sub, where, ids_in, weights_in, tok, grad, *refs):
-    packed, (table, far, ids, weights, both, staged, in_sems, sems) = refs[:sub], refs[sub:]
-    rows = tok.shape[0]
+    packed, refs = refs[:sub], refs[sub:]
+    far, table, ids, weights, both, staged, turned, far_staged, in_sems, sems = refs
+    rows, width = tok.shape
     loads = [
         pltpu.make_async_copy(ids_in, ids, in_sems.at[0]),
         pltpu.make_async_copy(weights_in, weights, in_sems.at[1]),
@@ -109,22 +115,30 @@
     table[0] = jnp.where(present > 0.5, lay.row(position, second), -1.0)
     table[1] = jnp.where(second, factor, 1.0)
     other = pl.ds(pl.multiple_of((1 - where[0]) * sub, sub), sub)
-    far[0] = table[0, other, :]
-    far[1] = table[1, other, :]
+    far_staged[rows:, :lanes] = table[0, other, :].astype(BF16)
+    far_staged[rows:, lanes : 2 * lanes] = table[1, other, :].astype(BF16)
+    far_staged[rows:, 2 * lanes :] = jnp.zeros((sub, width - 2 * lanes), BF16)
     loads[2].wait()
     loads[3].wait()
-    pairs = []
+    far_staged[:rows] = both[rows:]
+    send = pltpu.make_async_copy(far_staged, far, in_sems.at[4])
+    send.start()
     for offset in range(sub):
         row = pl.ds(where[0] * sub + (where[2] ^ offset), 1)
-        pairs.append((table[0, row, :], table[1, row, :]))
-    pack(pairs, both[...], lay.rows, staged, packed, sems)
-
-
-def relay_kernel(lay, where, far, tok, grad, packed, staged, sems):
-    both = jnp.concatenate([tok[...], grad[...]], axis=0)
-    sub = packed.shape[0]
-    pairs = [(far[0, e : e + 1], far[1, e : e + 1]) for e in range(sub)]
-    pack(pairs, both, lay.rows, staged, [packed.at[e] for e in range(sub)], sems)
+        turned[0, offset : offset + 1] = table[0, row, :]
+        turned[1, offset : offset + 1] = table[1, row, :]
+    pack(turned[0], turned[1], both[...], lay.rows, staged, packed, sems)
+    send.wait()
+
+
+def relay_kernel(lay, where, tok, far, packed, key, staged, sems):
+    rows = tok.shape[0]
+    lanes = key.shape[1]
+    both = jnp.concatenate([tok[...], far[:rows]], axis=0)
+    outs = [packed.at[e] for e in range(packed.shape[0])]
+    key[...] = far[rows:, :lanes].astype(F32)
+    factor = far[rows:, lanes : 2 * lanes].astype(F32)
+    pack(key[...], factor, both, lay.rows, staged, outs, sems)
 
 
 def split_sides(lay, got, first, second):
@@ -151,43 +165,28 @@
 def expert_kernel(lay, sub, direct, where, *refs):
     if direct:
         got, refs = refs[:sub], refs[sub:]
+        w_gate, w_up, down_in, *refs = refs
+        back_rows, refs = refs[:sub], refs[sub:]
     else:
-        got, refs = [refs[0].at[e] for e in range(sub)], refs[1:]
-    gate_in, up_in, down_in, back_rows, *kept = refs[:8]
-    w_gate, w_up, w_down, staged, first, second, small, down_small = refs[8:16]
-    in_sems, sems, kept_sems = refs[16:19]
-    loads = [
-        pltpu.make_async_copy(gate_in, w_gate, in_sems.at[0]),
-        pltpu.make_async_copy(up_in, w_up, in_sems.at[1]),
-        pltpu.make_async_copy(down_in, w_down, in_sems.at[2]),
-    ]
+        got, w_gate, w_up, down_in, back_rows, *refs = refs
+        got = [got.at[e] for e in range(sub)]
+        back_rows = [back_rows.at[e] for e in range(sub)]
+    kept, (staged, first, second, small, down_small, w_down) = refs[:4], refs[4:10]
+    kept_sems, sems, load_sem = refs[10:]
+    load = pltpu.make_async_copy(down_in, w_down, load_sem)
+    load.start()
     stores = [
         pltpu.make_async_copy(held, out, kept_sems.at[i])
         for i, (held, out) in enumerate(zip((first, second, small, down_small), kept))
     ]
     width, units = w_gate.shape
     total = sub * lay.side
-    if direct:
-        local, local_sems = refs[19:]
-        arrivals = [
-            pltpu.make_async_copy(got[e], local.at[e], local_sems.at[e]) for e in range(sub)
-        ]
-        for copy in arrivals + loads:
-            copy.start()
-        for copy in arrivals:
-            copy.wait()
-        got = [local.at[e] for e in range(sub)]
-    else:
-        for load in loads:
-            load.start()
     split_sides(lay, got, first, second)
     stores[0].start()
     stores[1].start()
-    loads[0].wait()
     gate = jnp.dot(first[...], w_gate[...], preferred_element_type=F32)
-    loads[1].wait()
     up = jnp.dot(first[...], w_up[...], preferred_element_type=F32)
-    loads[2].wait()
+    load.wait()
     back = jnp.dot(second[...], w_down[...], preferred_element_type=F32)
     back = align(lay, back, sub)
     slot = lax.broadcasted_iota(jnp.int32, (sub, lay.side, 128), 1).reshape(total, 128)
@@ -219,8 +218,7 @@
             staged[e, 2 * whole : lay.rows] = mixed.astype(BF16)
         staged[e, lay.rows :, :128] = jnp.broadcast_to(sums[e : e + 1], (8, 128)).astype(BF16)
         staged[e, lay.rows :, 128:] = jnp.zeros((8, half - 128), BF16)
-        target = (where[2] ^ e) if direct else e
-        copies.append(pltpu.make_async_copy(staged.at[e], back_rows.at[target], sems.at[e]))
+        copies.append(pltpu.make_async_copy(staged.at[e], back_rows[e], sems.at[e]))
         copies[-1].start()
     small[:, :units] = grad_gate
     small[:, units:] = grad_up
@@ -249,40 +247,51 @@
     for i in range(8):
         rows = pl.ds((i // 4) * total, total)
         loads.append(pltpu.make_async_copy(sources[i], held[i % 4].at[rows], sems.at[i]))
-        loads[-1].start()
-    for load in loads:
-        load.wait()
-    for b in range(replicas):
-        cols = slice(b * width, (b + 1) * width)
-        firsts[b] = first[:, cols]
-        seconds[b] = second[:, cols]
-    for s in reversed(range(replicas)):
-        b = lax.rem(where[1] + s, replicas)
-        outs[s][:, : 2 * units] = lax.dot_general(
-            firsts[b], small[...], ROWS_BY_ROWS, preferred_element_type=F32
-        ).astype(BF16)
-        outs[s][:, 2 * units :] = lax.dot_general(
-            seconds[b], down_small[...], ROWS_BY_ROWS, preferred_element_type=F32
-        ).astype(BF16)
+    for i in (0, 2, 4, 6, 1, 3, 5, 7):
+        loads[i].start()
+    for side, (rows_held, parts, factors, cols) in enumerate(
+        ((first, firsts, small, slice(0, 2 * units)),
+         (second, seconds, down_small, slice(2 * units, 3 * units)))
+    ):
+        for i in (side, side + 2, side + 4, side + 6):
+            loads[i].wait()
+        for b in range(replicas):
+            parts[b] = rows_held[:, b * width : (b + 1) * width]
+        for s in reversed(range(replicas)):
+            b = lax.rem(where[1] + s, replicas)
+            outs[s][:, cols] = lax.dot_general(
+                parts[b], factors[...], ROWS_BY_ROWS, preferred_element_type=F32
+            ).astype(BF16)
 
 
 def update_kernel(replicas, where, *refs):
     parts, moms, outs = refs[:replicas], refs[replicas : replicas + 3], refs[replicas + 3 :]
     outs, (held, made, in_sems, out_sems) = outs[:3], outs[3:]
     units = moms[0].shape[2]
-    loads = [pltpu.make_async_copy(moms[i].at[0], held.at[i], in_sems.at[i]) for i in range(3)]
-    stores = [pltpu.make_async_copy(made.at[i], outs[i].at[0], out_sems.at[i]) for i in range(3)]
-    for load in loads:
-        load.start()
+    pieces = 4 if moms[0].shape[1] % 32 == 0 else 1
+    step = moms[0].shape[1] // pieces
+    work = []
     for i in range(3):
+        for j in range(pieces):
+            rows = pl.ds(j * step, step)
+            sem = 4 * i + j
+            load = pltpu.make_async_copy(
+                moms[i].at[0, rows], held.at[i, rows], in_sems.at[sem]
+            )
+            load.start()
+            store = pltpu.make_async_copy(
+                made.at[i, rows], outs[i].at[0, rows], out_sems.at[sem]
+            )
+            work.append((i, slice(j * step, (j + 1) * step), load, store))
+    for i, rows, load, store in work:
         cols = slice(i * units, (i + 1) * units)
-        total = parts[0][:, cols].astype(F32)
+        total = parts[0][rows, cols].astype(F32)
         for part in parts[1:]:
-            total = total + part[:, cols].astype(F32)
-        loads[i].wait()
-        made[i] = 0.9 * held[i] + 0.1 * total
-        stores[i].start()
-    for store in stores:
+            total = total + part[rows, cols].astype(F32)
+        load.wait()
+        made[i, rows] = 0.9 * held[i, rows] + 0.1 * total
+        store.start()
+    for *_, store in work:
         store.wait()
 
 
@@ -304,28 +313,32 @@
     return value
 
 
-def partial_kernel(lay, rows, where, far, returned, out):
+def partial_kernel(lay, rows, where, key, returned, out):
     sub, _, half = returned.shape
-    lanes = far.shape[2]
-    total = gathered(far[0], returned[...])
+    lanes = key.shape[1]
+    total = gathered(key[...], returned[...])
     out[:rows, :half] = total[:rows].astype(BF16)
     out[:rows, half:] = total[rows:].astype(BF16)
-    out[rows:, :lanes] = route_values(lay, far[0], returned[...]).astype(BF16)
+    out[rows:, :lanes] = route_values(lay, key[...], returned[...]).astype(BF16)
     out[rows:, lanes:] = jnp.zeros((sub, 2 * half - lanes), BF16)
 
 
-def final_kernel(lay, where, table, returned, partial, ids, weights, out, route):
+def final_kernel(lay, sub, where, table, partial, ids, weights, *refs):
+    pieces, (out, route, returned, own) = refs[:sub], refs[sub:]
     rows, half = out.shape[0], returned.shape[2]
     topk = ids.shape[0]
-    sub = returned.shape[0]
-    own = table[0, pl.ds(pl.multiple_of(where[0] * sub, sub), sub), :]
-    total = gathered(own, returned[...])
+    for offset in range(sub):
+        returned[offset] = pieces[offset][...]
+        row = pl.ds(where[0] * sub + (where[2] ^ offset), 1)
+        own[offset : offset + 1] = table[0, row, :]
+    total = gathered(own[...], returned[...])
     out[:, :half] = (total[:rows] + partial[:rows, :half].astype(F32)).astype(BF16)
     out[:, half:] = (total[rows:] + partial[:rows, half:].astype(F32)).astype(BF16)
-    near = route_values(lay, own, returned[...])[:, :rows]
+    near = route_values(lay, own[...], returned[...])[:, :rows]
     far = partial[rows:, :rows].astype(F32)
     expert = lax.broadcasted_iota(jnp.int32, (sub, rows), 0)
-    near_expert, far_expert = expert + where[0] * sub, expert + (1 - where[0]) * sub
+    near_expert = (expert ^ where[2]) + where[0] * sub
+    far_expert = expert + (1 - where[0]) * sub
     for k in range(topk):
         name = ids[k : k + 1, :]
         picked = jnp.where(name == near_expert, near, 0.0)
@@ -369,12 +382,11 @@
     ids = route_ids.T
     weights = route_weights.T
     far_tok = across(tokens)
-    far_grad = across(out_grad)
     chunk = S((lay.rows, width), BF16)
     staged = pltpu.VMEM((sub, *chunk.shape), BF16)
-    *packed, table, far = call(
+    *packed, far, table = call(
         functools.partial(route_kernel, lay, sub),
-        [chunk] * sub + [S((2, experts, lanes), F32), S((2, sub, lanes), F32)],
+        [chunk] * sub + [S((rows + sub, width), BF16), S((2, experts, lanes), F32)],
         (where, ids, weights, tokens, out_grad),
         2 * sub * lay.rows * lanes * width,
         scratch=[
@@ -382,18 +394,22 @@
             pltpu.VMEM(weights.shape, weights.dtype),
             pltpu.VMEM((2 * rows, width), BF16),
             staged,
-            DMA((4,)),
+            pltpu.VMEM((2, sub, lanes), F32),
+            pltpu.VMEM((rows + sub, width), BF16),
+            DMA((5,)),
             DMA((sub,)),
         ],
         streamed=(1, 2, 3, 4),
-        out_streamed=range(sub),
+        out_streamed=range(sub + 1),
     )
     far = across(far)
-    got_a = packed[:1] + [permute(packed[offset], lambda i: i ^ offset) for offset in range(1, sub)]
-    (relayed,) = call(
+    got_a = packed[:1] + [None] * (sub - 1)
+    for offset in range(1, sub):
+        got_a[offset] = permute(packed[offset], lambda i: i ^ offset)
+    relayed, far_key = call(
         functools.partial(relay_kernel, lay),
-        [S((sub, *chunk.shape), BF16)],
-        (where, far, far_tok, far_grad),
+        [S((sub, *chunk.shape), BF16), S((sub, lanes), F32)],
+        (where, far_tok, far),
         2 * sub * lay.rows * lanes * width,
         scratch=[staged, DMA((sub,))],
         out_streamed=(0,),
@@ -401,26 +417,27 @@
     got_b = [within(relayed)]
 
     def expert(got, direct):
-        weight = pltpu.VMEM((width, units), BF16)
-        back = S((sub, lay.rows + 8, half), BF16)
+        back = (sub, lay.rows + 8, half)
         kept = [S((total, cols), BF16) for cols in (width, width, 2 * units, units)]
-        local = [pltpu.VMEM((sub, *chunk.shape), BF16), DMA((sub,))]
-        first_weight = len(got) + 1
-        return call(
+        outs = ([S(back[1:], BF16)] * sub if direct else [S(back, BF16)]) + kept
+        made = call(
             functools.partial(expert_kernel, lay, sub, direct),
-            [back] + kept,
+            outs,
             (where, *got, w_gate[0], w_up[0], w_down[0]),
             10 * total * width * units,
-            scratch=[weight, weight, weight, pltpu.VMEM(back.shape, BF16)]
+            scratch=[pltpu.VMEM(back, BF16)]
             + [pltpu.VMEM(x.shape, BF16) for x in kept]
-            + [DMA((3,)), DMA((sub,)), DMA((4,))]
-            + (local if direct else []),
-            streamed=range(1 if direct else first_weight, first_weight + 3),
-            out_streamed=range(5),
+            + [pltpu.VMEM((width, units), BF16), DMA((4,)), DMA((sub,)), DMA],
+            streamed=(len(got) + 3,),
+            out_streamed=range(len(outs)),
         )
-
-    back_a, *factors_a = expert(got_a, True)
-    back_b, *factors_b = expert(got_b, False)
+        return made[:-4], made[-4:]
+
+    back_a, factors_a = expert(got_a, True)
+    ret_a = [back_a[0]] + [None] * (sub - 1)
+    for offset in range(1, sub):
+        ret_a[offset] = permute(back_a[offset], lambda i: i ^ offset)
+    (back_b,), factors_b = expert(got_b, False)
     ret_b = within(back_b)
     turned = pltpu.VMEM((replicas, 2 * total, strip), BF16)
     parts = call(
@@ -442,25 +459,28 @@
     (partial,) = call(
         functools.partial(partial_kernel, lay, rows),
         [S((rows + sub, width), BF16)],
-        (where, far, ret_b),
+        (where, far_key, ret_b),
         2 * sub * lay.rows * lanes * half,
     )
     partial = across(partial)
-    ret_a = within(back_a)
     new = call(
         functools.partial(update_kernel, replicas),
         [S(mom_gate.shape, F32)] * 3,
         (where, parts[0], *moved, mom_gate, mom_up, mom_down),
         9 * strip * units,
-        scratch=[pltpu.VMEM((3, strip, units), F32)] * 2 + [DMA((3,)), DMA((3,))],
+        scratch=[pltpu.VMEM((3, strip, units), F32)] * 2 + [DMA((12,)), DMA((12,))],
         streamed=range(replicas + 1, replicas + 4),
         out_streamed=range(3),
     )
     grad_tokens, grad_route = call(
-        functools.partial(final_kernel, lay),
+        functools.partial(final_kernel, lay, sub),
         [S((rows, width), BF16), S((topk, rows), BF16)],
-        (where, table, ret_a, partial, ids, weights),
+        (where, table, partial, ids, weights, *ret_a),
         2 * sub * lay.rows * lanes * half,
+        scratch=[
+            pltpu.VMEM((sub, lay.rows + 8, half), BF16),
+            pltpu.VMEM((sub, lanes), F32),
+        ],
     )
     return (grad_tokens, grad_route.T, *new)
 

time: 103 us -> 102 us (level)
  waiting for transfers between devices: 24.6 us -> 43.9 us
  blocking collectives: 17.9 us -> 0 us
  starting transfers between devices: 28.1 us -> 34.4 us
  local copies, waits for them, and re-layouts: 5.93 us -> 0.09 us
  Pallas kernels: 25.1 us -> 22.6 us
    ppermute x11 -> x17, waiting for transfers between devices: 17.4 us -> 35.6 us  [permute(): return lax.ppermute(x, 'expert', [(i, partner(i)) for i in range(experts)])]
    all_to_all x1 -> x0, blocking collectives: 17.9 us -> none  [within(): lax.all_to_all(x, 'expert', split_axis=0, concat_axis=0, tiled=True, axis...]
    unnamed x46 -> x36, local copies, waits for them, and re-layouts: 5.93 us -> 0.09 us
    ppermute x11 -> x17, starting transfers between devices: 21 us -> 26.7 us  [permute(): return lax.ppermute(x, 'expert', [(i, partner(i)) for i in range(experts)])]
    pallas_call x8, Pallas kernels: 25.1 us -> 22.6 us  [call(): pl.pallas_call(kernel, out_shape=tuple(outs), in_specs=[SMEM] + [HBM if i...]
    all_to_all x2, waiting for transfers between devices: 7.23 us -> 8.26 us  [within(): lax.all_to_all(x, 'expert', split_axis=0, concat_axis=0, tiled=True, axis...]
  transfers between devices with their start and end apart: 14 -> 20, of which waited for: 5 -> 10; matrix products, arithmetic and copies ran while one was open for 0% -> 0% of each run, Pallas kernels for 15% -> 6%
where the time goes in v2:
time: 102 us
  waiting for transfers between devices  43.9 us (43%)
  starting transfers between devices  34.4 us (34%)
  Pallas kernels  22.6 us (22%)
    ppermute x17, waiting for transfers between devices, permute(): return lax.ppermute(x, 'expert', [(i, partner(i)) for i in range(experts)])  35.6 us
    ppermute x17, starting transfers between devices, permute(): return lax.ppermute(x, 'expert', [(i, partner(i)) for i in range(experts)])  26.7 us
    pallas_call x8, Pallas kernels, call(): pl.pallas_call(kernel, out_shape=tuple(outs), in_specs=[SMEM] + [HBM if i...  22.6 us
    all_to_all x2, waiting for transfers between devices, within(): lax.all_to_all(x, 'expert', split_axis=0, concat_axis=0, tiled=True, axis...  8.26 us
    all_to_all x2, starting transfers between devices, within(): lax.all_to_all(x, 'expert', split_axis=0, concat_axis=0, tiled=True, axis...  7.64 us
  transfers between devices with their start and end apart: 20, of which 10 were waited for; matrix products, arithmetic and copies ran while one was open for 0% of the time, Pallas kernels for 6%

profile of v2, /device:TPU:0, one launch (start us, length us, event | category | flops | bytes accessed | tf_op | source)
XLA Modules:
  0.0 101.9 jit_solution(4441228800183965769)
XLA Ops:
  0.7 0.1 pad_add_fusion.where
  0.7 2.9 %shard_map.137 = (bf16[56,1024]{1,0:T(8,128)(2,1)}, bf16[56,1024]{1,0:T(8,128)(2,1)}, bf16[56,1024]{1,0:T(8,128)(2,1)}, bf16[56,1024]{1,0:T(8,128)(2,1)}, bf16[5...) custom-call(s32[3]{0:T(128)S(1)} %pad_add_fusion.where, ...), custom_call_target="tpu_custom_call" | custom-call | flops 117440512 | bytes 1345792 | tf_op jit(solution)/shard_map/pallas_call | solution.py:31
  3.6 0.0 copy-start.10
  3.6 0.0 copy-start.9
  3.6 0.0 copy-start.8
  3.7 0.0 copy-start.7
  3.7 0.0 copy-start.3
  3.7 0.0 copy-start.4
  3.7 0.0 copy-start.5
  3.7 4.1 %collective-permute-start.1 = (bf16[72,1024]{1,0:T(8,128)(2,1)}, bf16[72,1024]{1,0:T(8,128)(2,1)S(1)}, u32[]{:S(2)}, u32[]{:S(2)}) collective-permute-start(bf16[72,1024]{1,0:T(8,128)(2,1)} %get-tuple-element.42), channel_id=1, source_target_pairs={{0,16},{2,18},{4,20},{6,22},{8,24},{10,26},{12,28},{14,30},{16,0},... | collective-permute-start | bytes 442376 | tf_op jit(solution)/shard_map/ppermute | solution.py:372
  7.8 0.1 collective-permute-start
  7.9 12.8 %collective-permute-done.tok = bf16[64,1024]{1,0:T(8,128)(2,1)S(1)} collective-permute-done((bf16[64,1024]{1,0:T(8,128)(2,1)}, bf16[64,1024]{1,0:T(8,128)(2,1)S(1)}, u32[]{:S(2)}, u32[]{:S(2)}) %collective-permute-start) | collective-permute-done | bytes 131104 | tf_op jit(solution)/shard_map/ppermute | solution.py:372
  20.7 0.0 collective-permute-done.1.far
  20.7 1.8 %shard_map.138 = (bf16[8,56,1024]{2,1,0:T(8,128)(2,1)}, f32[8,128]{1,0:T(8,128)S(1)}) custom-call(s32[3]{0:T(128)S(1)} %pad_add_fusion.where, bf16[64,1024]{1,0:T(8,128)(2,1)S(1)} %collective-permute-done.tok, bf16[72,1024]{1,0:T(8,128)(2,1)S(1)} %collective-permute-done.1.far), custom_call_target="tpu_custom_call" | custom-call | flops 117440512 | bytes 1200128 | tf_op jit(solution)/shard_map/pallas_call | solution.py:31
  22.5 4.0 %all-to-all-start = ((bf16[8,56,1024]{2,1,0:T(8,128)(2,1)}), bf16[8,56,1024]{2,1,0:T(8,128)(2,1)S(1)}, u32[]{:S(2)}, u32[]{:S(2)}) async-start(bf16[8,56,1024]{2,1,0:T(8,128)(2,1)} %get-tuple-element.44), calls=%async_computation | async-start | bytes 1835008 | tf_op jit(solution)/shard_map/all_to_all | solution.py:378
  26.5 2.0 %collective-permute-start.3 = (bf16[56,1024]{1,0:T(8,128)(2,1)}, bf16[56,1024]{1,0:T(8,128)(2,1)S(1)}, u32[]{:S(2)}, u32[]{:S(2)}) collective-permute-start(bf16[56,1024]{1,0:T(8,128)(2,1)} %get-tuple-element.47), channel_id=1, source_target_pairs={{0,2},{2,0},{4,6},{6,4},{8,10},{10,8},{12,14},{14,12},{16,18},{18,... | collective-permute-start | bytes 344072 | tf_op jit(solution)/shard_map/ppermute | solution.py:372
  28.5 1.5 %collective-permute-start.4 = (bf16[56,1024]{1,0:T(8,128)(2,1)}, bf16[56,1024]{1,0:T(8,128)(2,1)S(1)}, u32[]{:S(2)}, u32[]{:S(2)}) collective-permute-start(bf16[56,1024]{1,0:T(8,128)(2,1)} %get-tuple-element.48), channel_id=1, source_target_pairs={{0,4},{2,6},{4,0},{6,2},{8,12},{10,14},{12,8},{14,10},{16,20},{18,... | collective-permute-start | bytes 344072 | tf_op jit(solution)/shard_map/ppermute | solution.py:372
  30.0 0.0 collective-permute-start.5
  30.0 2.0 %collective-permute-start.6 = (bf16[56,1024]{1,0:T(8,128)(2,1)S(1)}, bf16[56,1024]{1,0:T(8,128)(2,1)S(1)}, u32[]{:S(2)}, u32[]{:S(2)}) collective-permute-start(bf16[56,1024]{1,0:T(8,128)(2,1)S(1)} %copy-done.9), channel_id=1, source_target_pairs={{0,8},{2,10},{4,12},{6,14},{8,0},{10,2},{12,4},{14,6},{16,24},{18,... | collective-permute-start | bytes 344072 | tf_op jit(solution)/shard_map/ppermute | solution.py:372
  32.0 0.0 copy-done.8
  32.0 1.5 %collective-permute-start.7 = (bf16[56,1024]{1,0:T(8,128)(2,1)S(1)}, bf16[56,1024]{1,0:T(8,128)(2,1)S(1)}, u32[]{:S(2)}, u32[]{:S(2)}) collective-permute-start(bf16[56,1024]{1,0:T(8,128)(2,1)S(1)} %copy-done.8), channel_id=1, source_target_pairs={{0,10},{2,8},{4,14},{6,12},{8,2},{10,0},{12,6},{14,4},{16,26},{18,... | collective-permute-start | bytes 344072 | tf_op jit(solution)/shard_map/ppermute | solution.py:372
  33.5 11.4 %collective-permute-done.3.refs_1_ = bf16[56,1024]{1,0:T(8,128)(2,1)S(1)} collective-permute-done((bf16[56,1024]{1,0:T(8,128)(2,1)}, bf16[56,1024]{1,0:T(8,128)(2,1)S(1)}, u32[]{:S(2)}, u32[]{:S(2)}) %collective-permute-start.3) | collective-permute-done | bytes 114720 | tf_op jit(solution)/shard_map/ppermute | solution.py:372
  44.8 0.2 collective-permute-start.8
  45.0 0.0 collective-permute-done.4.refs_2_
  45.0 0.0 copy-done.6
  45.0 1.8 %collective-permute-start.9 = (bf16[56,1024]{1,0:T(8,128)(2,1)S(1)}, bf16[56,1024]{1,0:T(8,128)(2,1)S(1)}, u32[]{:S(2)}, u32[]{:S(2)}) collective-permute-start(bf16[56,1024]{1,0:T(8,128)(2,1)S(1)} %copy-done.6), channel_id=1, source_target_pairs={{0,14},{2,12},{4,10},{6,8},{8,6},{10,4},{12,2},{14,0},{16,30},{18,... | collective-permute-start | bytes 344072 | tf_op jit(solution)/shard_map/ppermute | solution.py:372
  46.9 1.5 %collective-permute-done.5.refs_3_ = bf16[56,1024]{1,0:T(8,128)(2,1)S(1)} collective-permute-done((bf16[56,1024]{1,0:T(8,128)(2,1)S(1)}, bf16[56,1024]{1,0:T(8,128)(2,1)S(1)}, u32[]{:S(2)}, u32[]{:S(2)}) %collective-permute-start.5) | collective-permute-done | bytes 114720 | tf_op jit(solution)/shard_map/ppermute | solution.py:372
  48.4 0.0 collective-permute-done.6.refs_4_
  48.4 0.0 collective-permute-done.7.refs_5_
  48.4 3.2 %collective-permute-done.8.refs_6_ = bf16[56,1024]{1,0:T(8,128)(2,1)S(1)} collective-permute-done((bf16[56,1024]{1,0:T(8,128)(2,1)S(1)}, bf16[56,1024]{1,0:T(8,128)(2,1)S(1)}, u32[]{:S(2)}, u32[]{:S(2)}) %collective-permute-start.8) | collective-permute-done | bytes 114720 | tf_op jit(solution)/shard_map/ppermute | solution.py:372
  51.6 1.3 %collective-permute-done.9.refs_7_ = bf16[56,1024]{1,0:T(8,128)(2,1)S(1)} collective-permute-done((bf16[56,1024]{1,0:T(8,128)(2,1)S(1)}, bf16[56,1024]{1,0:T(8,128)(2,1)S(1)}, u32[]{:S(2)}, u32[]{:S(2)}) %collective-permute-start.9) | collective-permute-done | bytes 114720 | tf_op jit(solution)/shard_map/ppermute | solution.py:372
  53.0 0.0 copy-done.5
  53.0 3.9 %shard_map.141 = (bf16[64,512]{1,0:T(8,128)(2,1)}, bf16[64,512]{1,0:T(8,128)(2,1)}, bf16[64,512]{1,0:T(8,128)(2,1)}, bf16[64,512]{1,0:T(8,128)(2,1)}, bf16[64,51...) custom-call(s32[3]{0:T(128)S(1)} %pad_add_fusion.where, ...), custom_call_target="tpu_custom_call" | custom-call | flops 1006632960 | bytes 5439488 | tf_op jit(solution)/shard_map/pallas_call | solution.py:31
  56.9 0.0 all-to-all-done.refs_0_
  56.9 3.7 %shard_map.139 = (bf16[8,64,512]{2,1,0:T(8,128)(2,1)}, bf16[256,1024]{1,0:T(8,128)(2,1)}, bf16[256,1024]{1,0:T(8,128)(2,1)}, bf16[256,768]{1,0:T(8,128)(2,1)}, bf16[256,384]{1,0:T(8,128)(2,1)}) custom-call(s32[3]{0:T(128)S(1)} %pad_add_fusion.where, bf16[8,56,1024]{2,1,0:T(8,128)(2,1)S(1)} %all-to-all-done.refs_0_, bf16[1024,384]{1,0:T(8,128)(2,1)S(1)} %bitcast.14, ...), custom_call_target="tpu_custom_call" | custom-call | flops 1006632960 | bytes 5439488 | tf_op jit(solution)/shard_map/pallas_call | solution.py:31
  60.7 4.7 %shard_map.143 = (bf16[512,1152]{1,0:T(8,128)(2,1)S(1)}, bf16[512,1152]{1,0:T(8,128)(2,1)}) custom-call(s32[3]{0:T(128)S(1)} %pad_add_fusion.where, bf16[256,1024]{1,0:T(8,128)(2,1)} %get-tuple-element.64.refs_0_, bf16[256,1024]{1,0:T(8,128)(2,1)} %get-tuple-element.65.refs_1_, bf16[256,768]{1,0:T(8,128)(2,1)} %get-tuple-element.66.refs_2_, ...), custom_call_target="tpu_custom_call" | custom-call | flops 1207959552 | bytes 5636096 | tf_op jit(solution)/shard_map/pallas_call | solution.py:31
  65.4 0.0 copy-start
  65.4 0.0 copy-start.1
  65.4 0.0 copy-start.2
  65.5 0.1 collective-permute-start.17
  65.5 3.6 %all-to-all-start.1 = ((bf16[8,64,512]{2,1,0:T(8,128)(2,1)}), bf16[8,64,512]{2,1,0:T(8,128)(2,1)S(1)}, u32[]{:S(2)}, u32[]{:S(2)}) async-start(bf16[8,64,512]{2,1,0:T(8,128)(2,1)} %get-tuple-element.45), calls=%async_computation.1 | async-start | bytes 1048576 | tf_op jit(solution)/shard_map/all_to_all | solution.py:378
  69.2 1.9 %collective-permute-start.10 = (bf16[64,512]{1,0:T(8,128)(2,1)S(1)}, bf16[64,512]{1,0:T(8,128)(2,1)S(1)}, u32[]{:S(2)}, u32[]{:S(2)}) collective-permute-start(bf16[64,512]{1,0:T(8,128)(2,1)S(1)} %copy-done.17), channel_id=1, source_target_pairs={{0,2},{2,0},{4,6},{6,4},{8,10},{10,8},{12,14},{14,12},{16,18},{18,... | collective-permute-start | bytes 196616 | tf_op jit(solution)/shard_map/ppermute | solution.py:372
  71.1 8.3 %all-to-all-done.1.returned = bf16[8,64,512]{2,1,0:T(8,128)(2,1)S(1)} async-done(((bf16[8,64,512]{2,1,0:T(8,128)(2,1)}), bf16[8,64,512]{2,1,0:T(8,128)(2,1)S(1)}, u32[]{:S(2)}, u32[]{:S(2)}) %all-to-all-start.1) | async-done | bytes 524320 | tf_op jit(solution)/shard_map/all_to_all | solution.py:378
  79.4 0.8 shard_map.140
  80.2 3.3 %collective-permute-start.2 = (bf16[72,1024]{1,0:T(8,128)(2,1)S(1)}, bf16[72,1024]{1,0:T(8,128)(2,1)S(1)}, u32[]{:S(2)}, u32[]{:S(2)}) collective-permute-start(bf16[72,1024]{1,0:T(8,128)(2,1)S(1)} %shard_map.140), channel_id=1, source_target_pairs={{0,16},{2,18},{4,20},{6,22},{8,24},{10,26},{12,28},{14,30},{16,0},... | collective-permute-start | bytes 442376 | tf_op jit(solution)/shard_map/ppermute | solution.py:372
  83.6 0.6 collective-permute-start.11
  84.1 0.0 copy-done.15
  84.1 0.9 collective-permute-start.12
  85.0 0.0 collective-permute-done.10.refs_1_
  85.0 1.4 %collective-permute-start.13 = (bf16[64,512]{1,0:T(8,128)(2,1)S(1)}, bf16[64,512]{1,0:T(8,128)(2,1)S(1)}, u32[]{:S(2)}, u32[]{:S(2)}) collective-permute-start(bf16[64,512]{1,0:T(8,128)(2,1)S(1)} %copy-done.14), channel_id=1, source_target_pairs={{0,8},{2,10},{4,12},{6,14},{8,0},{10,2},{12,4},{14,6},{16,24},{18,... | collective-permute-start | bytes 196616 | tf_op jit(solution)/shard_map/ppermute | solution.py:372
  86.4 1.4 %collective-permute-done.11.refs_2_ = bf16[64,512]{1,0:T(8,128)(2,1)S(1)} collective-permute-done((bf16[64,512]{1,0:T(8,128)(2,1)S(1)}, bf16[64,512]{1,0:T(8,128)(2,1)S(1)}, u32[]{:S(2)}, u32[]{:S(2)}) %collective-permute-start.11) | collective-permute-done | bytes 65568 | tf_op jit(solution)/shard_map/ppermute | solution.py:372
  87.8 1.5 %collective-permute-start.14 = (bf16[64,512]{1,0:T(8,128)(2,1)S(1)}, bf16[64,512]{1,0:T(8,128)(2,1)S(1)}, u32[]{:S(2)}, u32[]{:S(2)}) collective-permute-start(bf16[64,512]{1,0:T(8,128)(2,1)S(1)} %copy-done.13), channel_id=1, source_target_pairs={{0,10},{2,8},{4,14},{6,12},{8,2},{10,0},{12,6},{14,4},{16,26},{18,... | collective-permute-start | bytes 196616 | tf_op jit(solution)/shard_map/ppermute | solution.py:372
  89.4 0.0 collective-permute-done.12.refs_3_
  89.4 1.7 %collective-permute-start.15 = (bf16[64,512]{1,0:T(8,128)(2,1)S(1)}, bf16[64,512]{1,0:T(8,128)(2,1)S(1)}, u32[]{:S(2)}, u32[]{:S(2)}) collective-permute-start(bf16[64,512]{1,0:T(8,128)(2,1)S(1)} %copy-done.12), channel_id=1, source_target_pairs={{0,12},{2,14},{4,8},{6,10},{8,4},{10,6},{12,0},{14,2},{16,28},{18,... | collective-permute-start | bytes 196616 | tf_op jit(solution)/shard_map/ppermute | solution.py:372
  91.1 0.0 collective-permute-done.13.refs_4_
  91.1 2.1 %collective-permute-start.16 = (bf16[64,512]{1,0:T(8,128)(2,1)S(1)}, bf16[64,512]{1,0:T(8,128)(2,1)S(1)}, u32[]{:S(2)}, u32[]{:S(2)}) collective-permute-start(bf16[64,512]{1,0:T(8,128)(2,1)S(1)} %copy-done.11), channel_id=1, source_target_pairs={{0,14},{2,12},{4,10},{6,8},{8,6},{10,4},{12,2},{14,0},{16,30},{18,... | collective-permute-start | bytes 196616 | tf_op jit(solution)/shard_map/ppermute | solution.py:372
  93.2 0.1 collective-permute-done.14.refs_5_
  93.3 1.6 %collective-permute-done.15.refs_6_ = bf16[64,512]{1,0:T(8,128)(2,1)S(1)} collective-permute-done((bf16[64,512]{1,0:T(8,128)(2,1)S(1)}, bf16[64,512]{1,0:T(8,128)(2,1)S(1)}, u32[]{:S(2)}, u32[]{:S(2)}) %collective-permute-start.15) | collective-permute-done | bytes 65568 | tf_op jit(solution)/shard_map/ppermute | solution.py:372
  94.9 2.3 %collective-permute-done.16.refs_7_ = bf16[64,512]{1,0:T(8,128)(2,1)S(1)} collective-permute-done((bf16[64,512]{1,0:T(8,128)(2,1)S(1)}, bf16[64,512]{1,0:T(8,128)(2,1)S(1)}, u32[]{:S(2)}, u32[]{:S(2)}) %collective-permute-start.16) | collective-permute-done | bytes 65568 | tf_op jit(solution)/shard_map/ppermute | solution.py:372
  97.2 0.0 collective-permute-done.2.partial
  97.2 0.0 copy-done.1
  97.2 1.5 %shard_map.142 = (bf16[64,1024]{1,0:T(8,128)(2,1)}, bf16[6,64]{1,0:T(8,128)(2,1)}) custom-call(s32[3]{0:T(128)S(1)} %pad_add_fusion.where, f32[2,16,128]{2,1,0:T(8,128)S(1)} %get-tuple-element.41.table, bf16[72,1024]{1,0:T(8,128)(2,1)S(1)} %collective-permute-done.2.partial, s32[6,64]{1,0:T(8,128)S(1)} %bitcast.10, bf16[6,64]{1,0:T(8,128)(2,1)S(1)} %bitcast.12, ...), custom_call_target="tpu_custom_call" | custom-call | flops 58720256 | bytes 822272 | tf_op jit(solution)/shard_map/pallas_call | solution.py:31
  98.7 0.0 collective-permute-done.17.refs_1_
  98.7 3.2 %shard_map.144 = (f32[1,512,384]{2,1,0:T(8,128)}, f32[1,512,384]{2,1,0:T(8,128)}, f32[1,512,384]{2,1,0:T(8,128)}) custom-call(s32[3]{0:T(128)S(1)} %pad_add_fusion.where, bf16[512,1152]{1,0:T(8,128)(2,1)S(1)} %get-tuple-element.72.refs_0_, bf16[512,1152]{1,0:T(8,128)(2,1)S(1)} %collective-permute-done.17.refs_1_, f32[1,512,384]{2,1,0:T(8,128)} %refs_2_.1, ...), custom_call_target="tpu_custom_call" | custom-call | flops 1769472 | bytes 7077888 | tf_op jit(solution)/shard_map/pallas_call | solution.py:31
  (21 shorter events, 0.0 us)
Async XLA Ops:
  3.6 26.4 %copy-start.10 = (bf16[56,1024]{1,0:T(8,128)(2,1)S(1)}, bf16[56,1024]{1,0:T(8,128)(2,1)}, u32[]{:S(2)}) copy-start(bf16[56,1024]{1,0:T(8,128)(2,1)} %get-tuple-element.49) | copy-start | bytes 344068
  3.6 26.4 %copy-start.9 = (bf16[56,1024]{1,0:T(8,128)(2,1)S(1)}, bf16[56,1024]{1,0:T(8,128)(2,1)}, u32[]{:S(2)}) copy-start(bf16[56,1024]{1,0:T(8,128)(2,1)} %get-tuple-element.50) | copy-start | bytes 344068
  3.6 28.4 %copy-start.8 = (bf16[56,1024]{1,0:T(8,128)(2,1)S(1)}, bf16[56,1024]{1,0:T(8,128)(2,1)}, u32[]{:S(2)}) copy-start(bf16[56,1024]{1,0:T(8,128)(2,1)} %get-tuple-element.51) | copy-start | bytes 344068
  3.7 41.2 %copy-start.7 = (bf16[56,1024]{1,0:T(8,128)(2,1)S(1)}, bf16[56,1024]{1,0:T(8,128)(2,1)}, u32[]{:S(2)}) copy-start(bf16[56,1024]{1,0:T(8,128)(2,1)} %get-tuple-element.52) | copy-start | bytes 344068
  3.7 41.4 %copy-start.6 = (bf16[56,1024]{1,0:T(8,128)(2,1)S(1)}, bf16[56,1024]{1,0:T(8,128)(2,1)}, u32[]{:S(2)}) copy-start(bf16[56,1024]{1,0:T(8,128)(2,1)} %get-tuple-element.53) | copy-start | bytes 344068
  3.7 49.3 %copy-start.3 = (bf16[1,1024,384]{2,1,0:T(8,128)(2,1)S(1)}, bf16[1,1024,384]{2,1,0:T(8,128)(2,1)}, u32[]{:S(2)}) copy-start(bf16[1,1024,384]{2,1,0:T(8,128)(2,1)} %param.14) | copy-start | bytes 2359300
  3.7 49.3 %copy-start.4 = (bf16[1,1024,384]{2,1,0:T(8,128)(2,1)S(1)}, bf16[1,1024,384]{2,1,0:T(8,128)(2,1)}, u32[]{:S(2)}) copy-start(bf16[1,1024,384]{2,1,0:T(8,128)(2,1)} %param.15) | copy-start | bytes 2359300
  3.7 49.3 %copy-start.5 = (bf16[56,1024]{1,0:T(8,128)(2,1)S(1)}, bf16[56,1024]{1,0:T(8,128)(2,1)}, u32[]{:S(2)}) copy-start(bf16[56,1024]{1,0:T(8,128)(2,1)} %get-tuple-element.46.refs_0_) | copy-start | bytes 344068
  3.7 17.0 %collective-permute-start.1 = (bf16[72,1024]{1,0:T(8,128)(2,1)}, bf16[72,1024]{1,0:T(8,128)(2,1)S(1)}, u32[]{:S(2)}, u32[]{:S(2)}) collective-permute-start(bf16[72,1024]{1,0:T(8,128)(2,1)} %get-tuple-element.42), channel_id=1, source_target_pairs={{0,16},{2,18},{4,20},{6,22},{8,24},{10,26},{12,28},{14,30},{16,0},... | collective-permute-start | bytes 442376 | tf_op jit(solution)/shard_map/ppermute | solution.py:372
  7.8 12.8 %collective-permute-start = (bf16[64,1024]{1,0:T(8,128)(2,1)}, bf16[64,1024]{1,0:T(8,128)(2,1)S(1)}, u32[]{:S(2)}, u32[]{:S(2)}) collective-permute-start(bf16[64,1024]{1,0:T(8,128)(2,1)} %tok.1), channel_id=1, source_target_pairs={{0,16},{2,18},{4,20},{6,22},{8,24},{10,26},{12,28},{14,30},{16,0},... | collective-permute-start | bytes 393224 | tf_op jit(solution)/shard_map/ppermute | solution.py:372
  22.5 34.4 %all-to-all-start = ((bf16[8,56,1024]{2,1,0:T(8,128)(2,1)}), bf16[8,56,1024]{2,1,0:T(8,128)(2,1)S(1)}, u32[]{:S(2)}, u32[]{:S(2)}) async-start(bf16[8,56,1024]{2,1,0:T(8,128)(2,1)} %get-tuple-element.44), calls=%async_computation | async-start | bytes 1835008 | tf_op jit(solution)/shard_map/all_to_all | solution.py:378
  26.5 18.3 %collective-permute-start.3 = (bf16[56,1024]{1,0:T(8,128)(2,1)}, bf16[56,1024]{1,0:T(8,128)(2,1)S(1)}, u32[]{:S(2)}, u32[]{:S(2)}) collective-permute-start(bf16[56,1024]{1,0:T(8,128)(2,1)} %get-tuple-element.47), channel_id=1, source_target_pairs={{0,2},{2,0},{4,6},{6,4},{8,10},{10,8},{12,14},{14,12},{16,18},{18,... | collective-permute-start | bytes 344072 | tf_op jit(solution)/shard_map/ppermute | solution.py:372
  28.5 16.5 %collective-permute-start.4 = (bf16[56,1024]{1,0:T(8,128)(2,1)}, bf16[56,1024]{1,0:T(8,128)(2,1)S(1)}, u32[]{:S(2)}, u32[]{:S(2)}) collective-permute-start(bf16[56,1024]{1,0:T(8,128)(2,1)} %get-tuple-element.48), channel_id=1, source_target_pairs={{0,4},{2,6},{4,0},{6,2},{8,12},{10,14},{12,8},{14,10},{16,20},{18,... | collective-permute-start | bytes 344072 | tf_op jit(solution)/shard_map/ppermute | solution.py:372
  30.0 18.4 %collective-permute-start.5 = (bf16[56,1024]{1,0:T(8,128)(2,1)S(1)}, bf16[56,1024]{1,0:T(8,128)(2,1)S(1)}, u32[]{:S(2)}, u32[]{:S(2)}) collective-permute-start(bf16[56,1024]{1,0:T(8,128)(2,1)S(1)} %copy-done.10), channel_id=1, source_target_pairs={{0,6},{2,4},{4,2},{6,0},{8,14},{10,12},{12,10},{14,8},{16,22},{18,... | collective-permute-start | bytes 344072 | tf_op jit(solution)/shard_map/ppermute | solution.py:372
  30.0 18.4 %collective-permute-start.6 = (bf16[56,1024]{1,0:T(8,128)(2,1)S(1)}, bf16[56,1024]{1,0:T(8,128)(2,1)S(1)}, u32[]{:S(2)}, u32[]{:S(2)}) collective-permute-start(bf16[56,1024]{1,0:T(8,128)(2,1)S(1)} %copy-done.9), channel_id=1, source_target_pairs={{0,8},{2,10},{4,12},{6,14},{8,0},{10,2},{12,4},{14,6},{16,24},{18,... | collective-permute-start | bytes 344072 | tf_op jit(solution)/shard_map/ppermute | solution.py:372
  32.0 16.4 %collective-permute-start.7 = (bf16[56,1024]{1,0:T(8,128)(2,1)S(1)}, bf16[56,1024]{1,0:T(8,128)(2,1)S(1)}, u32[]{:S(2)}, u32[]{:S(2)}) collective-permute-start(bf16[56,1024]{1,0:T(8,128)(2,1)S(1)} %copy-done.8), channel_id=1, source_target_pairs={{0,10},{2,8},{4,14},{6,12},{8,2},{10,0},{12,6},{14,4},{16,26},{18,... | collective-permute-start | bytes 344072 | tf_op jit(solution)/shard_map/ppermute | solution.py:372
  44.8 6.8 %collective-permute-start.8 = (bf16[56,1024]{1,0:T(8,128)(2,1)S(1)}, bf16[56,1024]{1,0:T(8,128)(2,1)S(1)}, u32[]{:S(2)}, u32[]{:S(2)}) collective-permute-start(bf16[56,1024]{1,0:T(8,128)(2,1)S(1)} %copy-done.7), channel_id=1, source_target_pairs={{0,12},{2,14},{4,8},{6,10},{8,4},{10,6},{12,0},{14,2},{16,28},{18,... | collective-permute-start | bytes 344072 | tf_op jit(solution)/shard_map/ppermute | solution.py:372
  45.0 7.9 %collective-permute-start.9 = (bf16[56,1024]{1,0:T(8,128)(2,1)S(1)}, bf16[56,1024]{1,0:T(8,128)(2,1)S(1)}, u32[]{:S(2)}, u32[]{:S(2)}) collective-permute-start(bf16[56,1024]{1,0:T(8,128)(2,1)S(1)} %copy-done.6), channel_id=1, source_target_pairs={{0,14},{2,12},{4,10},{6,8},{8,6},{10,4},{12,2},{14,0},{16,30},{18,... | collective-permute-start | bytes 344072 | tf_op jit(solution)/shard_map/ppermute | solution.py:372
  60.7 8.5 %copy-start.17 = (bf16[64,512]{1,0:T(8,128)(2,1)S(1)}, bf16[64,512]{1,0:T(8,128)(2,1)}, u32[]{:S(2)}) copy-start(bf16[64,512]{1,0:T(8,128)(2,1)} %get-tuple-element.55) | copy-start | bytes 196612
  65.4 18.2 %copy-start.16 = (bf16[64,512]{1,0:T(8,128)(2,1)S(1)}, bf16[64,512]{1,0:T(8,128)(2,1)}, u32[]{:S(2)}) copy-start(bf16[64,512]{1,0:T(8,128)(2,1)} %get-tuple-element.56) | copy-start | bytes 196612
  65.4 18.8 %copy-start.15 = (bf16[64,512]{1,0:T(8,128)(2,1)S(1)}, bf16[64,512]{1,0:T(8,128)(2,1)}, u32[]{:S(2)}) copy-start(bf16[64,512]{1,0:T(8,128)(2,1)} %get-tuple-element.57) | copy-start | bytes 196612
  65.4 19.6 %copy-start.14 = (bf16[64,512]{1,0:T(8,128)(2,1)S(1)}, bf16[64,512]{1,0:T(8,128)(2,1)}, u32[]{:S(2)}) copy-start(bf16[64,512]{1,0:T(8,128)(2,1)} %get-tuple-element.58) | copy-start | bytes 196612
  65.4 22.4 %copy-start.13 = (bf16[64,512]{1,0:T(8,128)(2,1)S(1)}, bf16[64,512]{1,0:T(8,128)(2,1)}, u32[]{:S(2)}) copy-start(bf16[64,512]{1,0:T(8,128)(2,1)} %get-tuple-element.59) | copy-start | bytes 196612
  65.4 24.0 %copy-start.12 = (bf16[64,512]{1,0:T(8,128)(2,1)S(1)}, bf16[64,512]{1,0:T(8,128)(2,1)}, u32[]{:S(2)}) copy-start(bf16[64,512]{1,0:T(8,128)(2,1)} %get-tuple-element.60) | copy-start | bytes 196612
  65.4 25.7 %copy-start.11 = (bf16[64,512]{1,0:T(8,128)(2,1)S(1)}, bf16[64,512]{1,0:T(8,128)(2,1)}, u32[]{:S(2)}) copy-start(bf16[64,512]{1,0:T(8,128)(2,1)} %get-tuple-element.61) | copy-start | bytes 196612
  65.4 31.8 %copy-start = (bf16[64,512]{1,0:T(8,128)(2,1)S(1)}, bf16[64,512]{1,0:T(8,128)(2,1)}, u32[]{:S(2)}) copy-start(bf16[64,512]{1,0:T(8,128)(2,1)} %get-tuple-element.54.refs_0_) | copy-start | bytes 196612
  65.4 31.7 %copy-start.1 = (s32[64,6]{0,1:T(8,128)S(1)}, s32[64,6]{0,1:T(8,128)}, u32[]{:S(2)}) copy-start(s32[64,6]{0,1:T(8,128)} %param.11) | copy-start | bytes 4612
  65.4 31.7 %copy-start.2 = (bf16[64,6]{0,1:T(8,128)(2,1)S(1)}, bf16[64,6]{0,1:T(8,128)(2,1)}, u32[]{:S(2)}) copy-start(bf16[64,6]{0,1:T(8,128)(2,1)} %param.12) | copy-start | bytes 2308
  65.5 33.2 %collective-permute-start.17 = (bf16[512,1152]{1,0:T(8,128)(2,1)}, bf16[512,1152]{1,0:T(8,128)(2,1)S(1)}, u32[]{:S(2)}, u32[]{:S(2)}) collective-permute-start(bf16[512,1152]{1,0:T(8,128)(2,1)} %get-tuple-element.73), channel_id=1, source_target_pairs={{0,1},{1,0},{2,3},{3,2},{4,5},{5,4},{6,7},{7,6},{8,9},{9,8},{10,11... | collective-permute-start | bytes 3538952 | tf_op jit(solution)/shard_map/ppermute | solution.py:454
  65.5 13.8 %all-to-all-start.1 = ((bf16[8,64,512]{2,1,0:T(8,128)(2,1)}), bf16[8,64,512]{2,1,0:T(8,128)(2,1)S(1)}, u32[]{:S(2)}, u32[]{:S(2)}) async-start(bf16[8,64,512]{2,1,0:T(8,128)(2,1)} %get-tuple-element.45), calls=%async_computation.1 | async-start | bytes 1048576 | tf_op jit(solution)/shard_map/all_to_all | solution.py:378
  69.2 15.8 %collective-permute-start.10 = (bf16[64,512]{1,0:T(8,128)(2,1)S(1)}, bf16[64,512]{1,0:T(8,128)(2,1)S(1)}, u32[]{:S(2)}, u32[]{:S(2)}) collective-permute-start(bf16[64,512]{1,0:T(8,128)(2,1)S(1)} %copy-done.17), channel_id=1, source_target_pairs={{0,2},{2,0},{4,6},{6,4},{8,10},{10,8},{12,14},{14,12},{16,18},{18,... | collective-permute-start | bytes 196616 | tf_op jit(solution)/shard_map/ppermute | solution.py:372
  80.2 16.9 %collective-permute-start.2 = (bf16[72,1024]{1,0:T(8,128)(2,1)S(1)}, bf16[72,1024]{1,0:T(8,128)(2,1)S(1)}, u32[]{:S(2)}, u32[]{:S(2)}) collective-permute-start(bf16[72,1024]{1,0:T(8,128)(2,1)S(1)} %shard_map.140), channel_id=1, source_target_pairs={{0,16},{2,18},{4,20},{6,22},{8,24},{10,26},{12,28},{14,30},{16,0},... | collective-permute-start | bytes 442376 | tf_op jit(solution)/shard_map/ppermute | solution.py:372
  83.6 4.3 %collective-permute-start.11 = (bf16[64,512]{1,0:T(8,128)(2,1)S(1)}, bf16[64,512]{1,0:T(8,128)(2,1)S(1)}, u32[]{:S(2)}, u32[]{:S(2)}) collective-permute-start(bf16[64,512]{1,0:T(8,128)(2,1)S(1)} %copy-done.16), channel_id=1, source_target_pairs={{0,4},{2,6},{4,0},{6,2},{8,12},{10,14},{12,8},{14,10},{16,20},{18,... | collective-permute-start | bytes 196616 | tf_op jit(solution)/shard_map/ppermute | solution.py:372
  84.1 5.2 %collective-permute-start.12 = (bf16[64,512]{1,0:T(8,128)(2,1)S(1)}, bf16[64,512]{1,0:T(8,128)(2,1)S(1)}, u32[]{:S(2)}, u32[]{:S(2)}) collective-permute-start(bf16[64,512]{1,0:T(8,128)(2,1)S(1)} %copy-done.15), channel_id=1, source_target_pairs={{0,6},{2,4},{4,2},{6,0},{8,14},{10,12},{12,10},{14,8},{16,22},{18,... | collective-permute-start | bytes 196616 | tf_op jit(solution)/shard_map/ppermute | solution.py:372
  85.0 6.1 %collective-permute-start.13 = (bf16[64,512]{1,0:T(8,128)(2,1)S(1)}, bf16[64,512]{1,0:T(8,128)(2,1)S(1)}, u32[]{:S(2)}, u32[]{:S(2)}) collective-permute-start(bf16[64,512]{1,0:T(8,128)(2,1)S(1)} %copy-done.14), channel_id=1, source_target_pairs={{0,8},{2,10},{4,12},{6,14},{8,0},{10,2},{12,4},{14,6},{16,24},{18,... | collective-permute-start | bytes 196616 | tf_op jit(solution)/shard_map/ppermute | solution.py:372
  87.8 5.4 %collective-permute-start.14 = (bf16[64,512]{1,0:T(8,128)(2,1)S(1)}, bf16[64,512]{1,0:T(8,128)(2,1)S(1)}, u32[]{:S(2)}, u32[]{:S(2)}) collective-permute-start(bf16[64,512]{1,0:T(8,128)(2,1)S(1)} %copy-done.13), channel_id=1, source_target_pairs={{0,10},{2,8},{4,14},{6,12},{8,2},{10,0},{12,6},{14,4},{16,26},{18,... | collective-permute-start | bytes 196616 | tf_op jit(solution)/shard_map/ppermute | solution.py:372
  89.4 5.5 %collective-permute-start.15 = (bf16[64,512]{1,0:T(8,128)(2,1)S(1)}, bf16[64,512]{1,0:T(8,128)(2,1)S(1)}, u32[]{:S(2)}, u32[]{:S(2)}) collective-permute-start(bf16[64,512]{1,0:T(8,128)(2,1)S(1)} %copy-done.12), channel_id=1, source_target_pairs={{0,12},{2,14},{4,8},{6,10},{8,4},{10,6},{12,0},{14,2},{16,28},{18,... | collective-permute-start | bytes 196616 | tf_op jit(solution)/shard_map/ppermute | solution.py:372
  91.1 6.1 %collective-permute-start.16 = (bf16[64,512]{1,0:T(8,128)(2,1)S(1)}, bf16[64,512]{1,0:T(8,128)(2,1)S(1)}, u32[]{:S(2)}, u32[]{:S(2)}) collective-permute-start(bf16[64,512]{1,0:T(8,128)(2,1)S(1)} %copy-done.11), channel_id=1, source_target_pairs={{0,14},{2,12},{4,10},{6,8},{8,6},{10,4},{12,2},{14,0},{16,30},{18,... | collective-permute-start | bytes 196616 | tf_op jit(solution)/shard_map/ppermute | solution.py:372
